TPU v7x, 256 devices: a whole 4x4x8 slice. The times are simulated.
256 devices in a mesh: leaf: 128 (over y, x, z), rhs: 2 (over core).
Axes of the slice: x: 4, y: 4, z: 8, core: 2. Of those that a mesh axis runs over, the one named last changes fastest.
Arguments:
- rhs_block: bfloat16 [2048, 128, 256], P('leaf', 'rhs'), may hold values from -6 to 6
- basis: bfloat16 [2048, 256, 256], P(('leaf', 'rhs')), may hold values from -0.375 to 0.375
- red_inverse: bfloat16 [2048, 192, 192], P(('leaf', 'rhs')), may hold values from -0.4375 to 0.4375
- forward_coupling: bfloat16 [2048, 64, 1536], P(('leaf', 'rhs')), may hold values from -0.15625 to 0.15625
- backward_coupling: bfloat16 [2048, 192, 512], P(('leaf', 'rhs')), may hold values from -0.25 to 0.25
- parent_inverse: bfloat16 [1024, 128, 128], P(('leaf', 'rhs')), may hold values from -0.5 to 0.5
- near_index: int32 [2048, 8], P('leaf'), may hold values from 0 to 2047, as said below
- near_count: int32 [2048], P('leaf'), may hold values from 1 to 8, as said below
Outputs:
- solution: bfloat16 [2048, 128, 256], P('leaf', 'rhs')
Inputs may be any that keep to these rules, and one draw needn't show every extreme that they name: `near_index`: every slot, used or not, names a cluster other than its own whose distance from it in tree order is at most 32; some slot in every draw is at distance 32. Slots k >= near_count[c] of cluster c are unused.
All inputs are finite; a program needn't handle non-finite values.
Results may differ from a plain program's by a relative error of at most 0.007.
Values may be sent and summed in bfloat16 or wider, within the bound.
No kernel may reach another device: no remote copies, remote signals or barrier semaphores. Data moves between devices by JAX's collectives and lax.ppermute only.
A program may use at most 64 MiB of HBM per device.

v0:
```python
import jax
import jax.numpy as jnp
from jax import lax
from jax.sharding import PartitionSpec as P

CL_DEV = 16


def passed_along(value, axis, steps):
    count = lax.axis_size(axis)
    leading, last = (max(0, -steps), min(count, count - steps))
    return lax.ppermute(value, axis, [(source, source + steps) for source in range(leading, last)])


def rounded(values):
    return values.astype(jnp.bfloat16)


def fetch_redundant(values, distance):
    moved = passed_along(values, ("leaf", "rhs"), distance)
    return moved


def fetch_skeleton(values, distance):
    moved = passed_along(values, ("leaf", "rhs"), distance)
    return moved


def neighbourhood(values, reach_devices, fetcher):
    lower_side = [fetcher(values, distance) for distance in range(reach_devices, 0, -1)]
    upper_side = [fetcher(values, -distance) for distance in range(1, reach_devices + 1)]
    return jnp.concatenate(lower_side + [values] + upper_side, axis=0)


def collect(window, indices, in_use):
    picked = jnp.take(window, indices.reshape(-1), axis=0)
    picked = picked.reshape(indices.shape + window.shape[1:])
    return jnp.where(in_use[:, :, None, None], picked, jnp.zeros((), picked.dtype))


def on_device(
    rhs_block,
    basis,
    red_inverse,
    forward_coupling,
    backward_coupling,
    parent_inverse,
    near_index,
    near_count,
):
    single = jnp.float32
    right_side = lax.all_to_all(rhs_block, "rhs", split_axis=0, concat_axis=1, tiled=True)
    owned_rows = right_side.shape[0]
    offset = lax.axis_index("rhs") * owned_rows
    indices = lax.dynamic_slice_in_dim(near_index, offset, owned_rows, 0)
    counts = lax.dynamic_slice_in_dim(near_count, offset, owned_rows, 0)
    position = lax.axis_index(("leaf", "rhs")) * owned_rows
    basis_all, inverse_all, forward_all, backward_all, parent_all = (
        basis,
        red_inverse,
        forward_coupling,
        backward_coupling,
        parent_inverse,
    )
    reach_devices = 2 * CL_DEV // owned_rows
    skeleton = parent_inverse.shape[1] // 2
    redundant_rows = red_inverse.shape[1]
    slot_count = near_index.shape[1]
    columns = right_side.shape[1]
    projected = jnp.einsum("cna,cab->cnb", right_side, basis_all, preferred_element_type=single)
    eliminated = rounded(
        jnp.einsum(
            "cnr,cqr->cnq",
            rounded(projected[..., :redundant_rows]),
            inverse_all,
            preferred_element_type=single,
        )
    )
    in_use = jnp.arange(slot_count, dtype=jnp.int32)[None, :] < counts[:, None]
    relative = indices - position + reach_devices * owned_rows
    window = neighbourhood(eliminated, reach_devices, fetch_redundant)
    near_redundant = collect(window, relative, in_use)
    forward_blocks = forward_all.reshape(owned_rows, skeleton, slot_count, redundant_rows)
    update = jnp.einsum(
        "ckna,cqka->cnq", near_redundant, forward_blocks, preferred_element_type=single
    )
    reduced = rounded(projected[..., redundant_rows:] - update)
    paired = jnp.concatenate([reduced[0::2], reduced[1::2]], axis=-1)
    solved = rounded(jnp.einsum("pnq,pmq->pnm", paired, parent_all, preferred_element_type=single))
    skeleton_part = jnp.stack([solved[..., :skeleton], solved[..., skeleton:]], axis=1).reshape(
        owned_rows, columns, skeleton
    )
    window_skeleton = neighbourhood(skeleton_part, reach_devices, fetch_skeleton)
    near_skeleton = collect(window_skeleton, relative, in_use)
    backward_blocks = backward_all.reshape(owned_rows, redundant_rows, slot_count, skeleton)
    carried = jnp.einsum(
        "ckna,crka->cnr", near_skeleton, backward_blocks, preferred_element_type=single
    )
    corrected = rounded(eliminated.astype(single) - carried)
    recovered = rounded(
        jnp.einsum("cnq,cqr->cnr", corrected, inverse_all, preferred_element_type=single)
    )
    combined = jnp.concatenate([recovered, skeleton_part], axis=-1)
    solution = rounded(
        jnp.einsum("cnb,cab->cna", combined, basis_all, preferred_element_type=single)
    )
    solution = lax.all_to_all(solution, "rhs", split_axis=1, concat_axis=0, tiled=True)
    return solution


def solution(mesh):
    in_specs = (
        P("leaf", "rhs", None),
        P(("leaf", "rhs"), None, None),
        P(("leaf", "rhs"), None, None),
        P(("leaf", "rhs"), None, None),
        P(("leaf", "rhs"), None, None),
        P(("leaf", "rhs"), None, None),
        P("leaf", None),
        P("leaf"),
    )
    out_specs = P("leaf", "rhs", None)
    return jax.shard_map(
        on_device, mesh=mesh, in_specs=in_specs, out_specs=out_specs, check_vma=False
    )
```

profile of v0, /device:TPU:9, one launch (start us, length us, event | category | flops | bytes accessed | tf_op | source)
XLA Modules:
  0.0 139.6 jit_solution(6370671450037310618)
XLA Ops:
  0.0 5.6 %all_to_all.36 = bf16[16,64,256]{2,1,0:T(8,128)(2,1)S(1)} all-to-all(bf16[16,64,256]{2,1,0:T(8,128)(2,1)} %param.8), channel_id=1, replica_groups=mesh['leaf'=128,'rhs'=2] {'rhs'}, dimensions={0} | all-to-all | bytes 1048576 | tf_op jit(solution)/shard_map/all_to_all | solution.py:52
  5.7 0.3 fusion.55
  6.0 0.7 copy-done.3
  6.8 0.4 convolution_convert_fusion.2
  7.2 4.9 %collective-permute-start = (bf16[8,128,192]{1,2,0:T(8,128)(2,1)S(1)}, bf16[8,128,192]{1,2,0:T(8,128)(2,1)}, u32[]{:S(2)}, u32[]{:S(2)}) collective-permute-start(bf16[8,128,192]{1,2,0:T(8,128)(2,1)S(1)} %convolution_convert_fusion.2), channel_id=1, source_target_pairs={{0,4},{1,5},{2,6},{3,7},{4,8},{5,9},{6,10},{7,11},{8,12},{9,13},{1... | collective-permute-start | bytes 1179656 | tf_op jit(solution)/shard_map/ppermute | solution.py:12
  12.1 6.7 %collective-permute-start.1 = (bf16[8,128,192]{1,2,0:T(8,128)(2,1)S(1)}, bf16[8,128,192]{1,2,0:T(8,128)(2,1)}, u32[]{:S(2)}, u32[]{:S(2)}) collective-permute-start(bf16[8,128,192]{1,2,0:T(8,128)(2,1)S(1)} %convolution_convert_fusion.2), channel_id=1, source_target_pairs={{0,3},{1,4},{2,5},{3,6},{4,7},{5,8},{6,9},{7,10},{8,11},{9,12},{10... | collective-permute-start | bytes 1179656 | tf_op jit(solution)/shard_map/ppermute | solution.py:12
  18.7 2.6 %collective-permute-start.2 = (bf16[8,128,192]{1,2,0:T(8,128)(2,1)S(1)}, bf16[8,128,192]{1,2,0:T(8,128)(2,1)}, u32[]{:S(2)}, u32[]{:S(2)}) collective-permute-start(bf16[8,128,192]{1,2,0:T(8,128)(2,1)S(1)} %convolution_convert_fusion.2), channel_id=1, source_target_pairs={{0,2},{1,3},{2,4},{3,5},{4,6},{5,7},{6,8},{7,9},{8,10},{9,11},{10,... | collective-permute-start | bytes 1179656 | tf_op jit(solution)/shard_map/ppermute | solution.py:12
  21.4 2.2 %collective-permute-start.3 = (bf16[8,128,192]{1,2,0:T(8,128)(2,1)S(1)}, bf16[8,128,192]{1,2,0:T(8,128)(2,1)S(1)}, u32[]{:S(2)}, u32[]{:S(2)}) collective-permute-start(bf16[8,128,192]{1,2,0:T(8,128)(2,1)S(1)} %convolution_convert_fusion.2), channel_id=1, source_target_pairs={{0,1},{1,2},{2,3},{3,4},{4,5},{5,6},{6,7},{7,8},{8,9},{9,10},{10,1... | collective-permute-start | bytes 1179656 | tf_op jit(solution)/shard_map/ppermute | solution.py:12
  23.6 2.1 %collective-permute-start.4 = (bf16[8,128,192]{1,2,0:T(8,128)(2,1)S(1)}, bf16[8,128,192]{1,2,0:T(8,128)(2,1)S(1)}, u32[]{:S(2)}, u32[]{:S(2)}) collective-permute-start(bf16[8,128,192]{1,2,0:T(8,128)(2,1)S(1)} %convolution_convert_fusion.2), channel_id=1, source_target_pairs={{1,0},{2,1},{3,2},{4,3},{5,4},{6,5},{7,6},{8,7},{9,8},{10,9},{11,1... | collective-permute-start | bytes 1179656 | tf_op jit(solution)/shard_map/ppermute | solution.py:12
  26.2 0.1 compare_and_fusion
  26.2 0.1 copy.30
  26.3 4.3 %reshape.75 = bf16[8,64,8,192]{3,2,1,0:T(8,128)(2,1)} reshape(bf16[8,64,1536]{2,1,0:T(8,128)(2,1)} %param.11) | data formatting | bytes 3145728 | tf_op jit(solution)/shard_map/reshape | solution.py:83
  30.6 9.3 %collective-permute-start.5 = (bf16[8,128,192]{1,2,0:T(8,128)(2,1)S(1)}, bf16[8,128,192]{1,2,0:T(8,128)(2,1)S(1)}, u32[]{:S(2)}, u32[]{:S(2)}) collective-permute-start(bf16[8,128,192]{1,2,0:T(8,128)(2,1)S(1)} %convolution_convert_fusion.2), channel_id=1, source_target_pairs={{2,0},{3,1},{4,2},{5,3},{6,4},{7,5},{8,6},{9,7},{10,8},{11,9},{12,... | collective-permute-start | bytes 1179656 | tf_op jit(solution)/shard_map/ppermute | solution.py:12
  39.9 1.8 %constant_dynamic-update-slice_fusion.8 = bf16[72,128,192]{1,2,0:T(8,128)(2,1)} fusion(bf16[8,128,192]{1,2,0:T(8,128)(2,1)} %collective-permute-done), kind=kLoop, calls=%fused_computation.45 | loop fusion | bytes 786432
  41.7 6.1 %collective-permute-done.1 = bf16[8,128,192]{1,2,0:T(8,128)(2,1)} collective-permute-done((bf16[8,128,192]{1,2,0:T(8,128)(2,1)S(1)}, bf16[8,128,192]{1,2,0:T(8,128)(2,1)}, u32[]{:S(2)}, u32[]{:S(2)}) %collective-permute-start.1) | collective-permute-done | bytes 393248 | tf_op jit(solution)/shard_map/ppermute | solution.py:12
  47.8 3.7 %collective-permute-start.6 = (bf16[8,128,192]{1,2,0:T(8,128)(2,1)S(1)}, bf16[8,128,192]{1,2,0:T(8,128)(2,1)S(1)}, u32[]{:S(2)}, u32[]{:S(2)}) collective-permute-start(bf16[8,128,192]{1,2,0:T(8,128)(2,1)S(1)} %convolution_convert_fusion.2), channel_id=1, source_target_pairs={{3,0},{4,1},{5,2},{6,3},{7,4},{8,5},{9,6},{10,7},{11,8},{12,9},{13... | collective-permute-start | bytes 1179656 | tf_op jit(solution)/shard_map/ppermute | solution.py:12
  51.6 1.8 %constant_dynamic-update-slice_fusion.7 = bf16[72,128,192]{1,2,0:T(8,128)(2,1)} fusion(bf16[72,128,192]{1,2,0:T(8,128)(2,1)} %constant_dynamic-update-slice_fusion.8, bf16[8,128,192]{1,2,0:T(8,128)(2,1)} %collective-permute-done.1), kind=kLoop, calls=%fused_computation.44 | loop fusion | bytes 786432
  53.3 2.1 %collective-permute-done.2 = bf16[8,128,192]{1,2,0:T(8,128)(2,1)} collective-permute-done((bf16[8,128,192]{1,2,0:T(8,128)(2,1)S(1)}, bf16[8,128,192]{1,2,0:T(8,128)(2,1)}, u32[]{:S(2)}, u32[]{:S(2)}) %collective-permute-start.2) | collective-permute-done | bytes 393248 | tf_op jit(solution)/shard_map/ppermute | solution.py:12
  55.4 4.2 %collective-permute-start.7 = (bf16[8,128,192]{1,2,0:T(8,128)(2,1)S(1)}, bf16[8,128,192]{1,2,0:T(8,128)(2,1)S(1)}, u32[]{:S(2)}, u32[]{:S(2)}) collective-permute-start(bf16[8,128,192]{1,2,0:T(8,128)(2,1)S(1)} %convolution_convert_fusion.2), channel_id=1, source_target_pairs={{4,0},{5,1},{6,2},{7,3},{8,4},{9,5},{10,6},{11,7},{12,8},{13,9},{1... | collective-permute-start | bytes 1179656 | tf_op jit(solution)/shard_map/ppermute | solution.py:12
  59.7 1.8 %constant_dynamic-update-slice_fusion.6 = bf16[72,128,192]{1,2,0:T(8,128)(2,1)} fusion(bf16[72,128,192]{1,2,0:T(8,128)(2,1)} %constant_dynamic-update-slice_fusion.7, bf16[8,128,192]{1,2,0:T(8,128)(2,1)} %collective-permute-done.2), kind=kLoop, calls=%fused_computation.43 | loop fusion | bytes 786432
  61.5 0.8 constant_dynamic-update-slice_fusion.5
  62.3 0.8 constant_dynamic-update-slice_fusion.4
  63.1 0.8 constant_dynamic-update-slice_fusion.3
  63.9 0.8 constant_dynamic-update-slice_fusion.2
  64.7 8.2 %collective-permute-done.6 = bf16[8,128,192]{1,2,0:T(8,128)(2,1)S(1)} collective-permute-done((bf16[8,128,192]{1,2,0:T(8,128)(2,1)S(1)}, bf16[8,128,192]{1,2,0:T(8,128)(2,1)S(1)}, u32[]{:S(2)}, u32[]{:S(2)}) %collective-permute-start.6) | collective-permute-done | bytes 393248 | tf_op jit(solution)/shard_map/ppermute | solution.py:12
  72.8 0.8 constant_dynamic-update-slice_fusion.1
  73.6 7.0 %collective-permute-done.7 = bf16[8,128,192]{1,2,0:T(8,128)(2,1)S(1)} collective-permute-done((bf16[8,128,192]{1,2,0:T(8,128)(2,1)S(1)}, bf16[8,128,192]{1,2,0:T(8,128)(2,1)S(1)}, u32[]{:S(2)}, u32[]{:S(2)}) %collective-permute-start.7) | collective-permute-done | bytes 393248 | tf_op jit(solution)/shard_map/ppermute | solution.py:12
  80.6 0.8 constant_dynamic-update-slice_fusion
  81.4 4.6 %gather_fusion = bf16[64,128,192]{1,2,0:T(8,128)(2,1)} fusion(bf16[72,128,192]{1,2,0:T(8,128)(2,1)} %constant_dynamic-update-slice_fusion, s32[1024]{0:T(1024)S(1)} %pad_clamp_fusion), kind=kCustom, calls=%fused_computation | custom fusion | bytes 6291712 | tf_op jit(solution)/shard_map/jit(_take)/gather | solution.py:36
  86.0 4.3 %fusion.20 = bf16[8,128,64]{2,1,0:T(8,128)(2,1)S(1)} fusion(bf16[8,64,8,192]{3,2,1,0:T(8,128)(2,1)} %reshape.75, bf16[8,8,128,192]{2,3,1,0:T(8,128)(2,1)} %bitcast.40, pred[8,8]{1,0:T(8,128)(4,1)S(1)} %copy.30, pred[8,8]{1,0:T(8,128)(4,1)S(1)} %iota_compare_fusion, f32[8,128,256]{2,1,0:T(8,128)S(1)} %fusion.55), kind=kOutput, calls=%fused_computation.18 | convolution fusion | flops 204603392 | bytes 5111936 | tf_op jit(solution)/shard_map/ckna,cqka->cnq/dot_general | solution.py:84
  90.4 0.3 convolution_convert_fusion.3
  90.8 4.3 %collective-permute-start.8 = (bf16[8,128,64]{1,2,0:T(8,128)(2,1)S(1)}, bf16[8,128,64]{1,2,0:T(8,128)(2,1)S(1)}, u32[]{:S(2)}, u32[]{:S(2)}) collective-permute-start(bf16[8,128,64]{1,2,0:T(8,128)(2,1)S(1)} %bitcast.46), channel_id=1, source_target_pairs={{0,4},{1,5},{2,6},{3,7},{4,8},{5,9},{6,10},{7,11},{8,12},{9,13},{1... | collective-permute-start | bytes 393224 | tf_op jit(solution)/shard_map/ppermute | solution.py:12
  95.1 4.1 %collective-permute-start.9 = (bf16[8,128,64]{1,2,0:T(8,128)(2,1)S(1)}, bf16[8,128,64]{1,2,0:T(8,128)(2,1)S(1)}, u32[]{:S(2)}, u32[]{:S(2)}) collective-permute-start(bf16[8,128,64]{1,2,0:T(8,128)(2,1)S(1)} %bitcast.47), channel_id=1, source_target_pairs={{0,3},{1,4},{2,5},{3,6},{4,7},{5,8},{6,9},{7,10},{8,11},{9,12},{10... | collective-permute-start | bytes 393224 | tf_op jit(solution)/shard_map/ppermute | solution.py:12
  99.2 2.4 %copy.36 = bf16[8,192,512]{1,2,0:T(8,128)(2,1)} copy(bf16[8,192,512]{2,1,0:T(8,128)(2,1)S(1)} %copy-done.1) | data formatting | bytes 3145728 | tf_op args[4]
  101.6 1.9 %collective-permute-start.10 = (bf16[8,128,64]{1,2,0:T(8,128)(2,1)S(1)}, bf16[8,128,64]{1,2,0:T(8,128)(2,1)S(1)}, u32[]{:S(2)}, u32[]{:S(2)}) collective-permute-start(bf16[8,128,64]{1,2,0:T(8,128)(2,1)S(1)} %bitcast.48), channel_id=1, source_target_pairs={{0,2},{1,3},{2,4},{3,5},{4,6},{5,7},{6,8},{7,9},{8,10},{9,11},{10,... | collective-permute-start | bytes 393224 | tf_op jit(solution)/shard_map/ppermute | solution.py:12
  103.5 2.5 %collective-permute-start.11 = (bf16[8,128,64]{1,2,0:T(8,128)(2,1)S(1)}, bf16[8,128,64]{1,2,0:T(8,128)(2,1)S(1)}, u32[]{:S(2)}, u32[]{:S(2)}) collective-permute-start(bf16[8,128,64]{1,2,0:T(8,128)(2,1)S(1)} %bitcast.49), channel_id=1, source_target_pairs={{0,1},{1,2},{2,3},{3,4},{4,5},{5,6},{6,7},{7,8},{8,9},{9,10},{10,1... | collective-permute-start | bytes 393224 | tf_op jit(solution)/shard_map/ppermute | solution.py:12
  106.0 1.9 %collective-permute-start.12 = (bf16[8,128,64]{1,2,0:T(8,128)(2,1)S(1)}, bf16[8,128,64]{1,2,0:T(8,128)(2,1)S(1)}, u32[]{:S(2)}, u32[]{:S(2)}) collective-permute-start(bf16[8,128,64]{1,2,0:T(8,128)(2,1)S(1)} %bitcast.50), channel_id=1, source_target_pairs={{1,0},{2,1},{3,2},{4,3},{5,4},{6,5},{7,6},{8,7},{9,8},{10,9},{11,1... | collective-permute-start | bytes 393224 | tf_op jit(solution)/shard_map/ppermute | solution.py:12
  108.0 7.5 %collective-permute-start.13 = (bf16[8,128,64]{1,2,0:T(8,128)(2,1)S(1)}, bf16[8,128,64]{1,2,0:T(8,128)(2,1)S(1)}, u32[]{:S(2)}, u32[]{:S(2)}) collective-permute-start(bf16[8,128,64]{1,2,0:T(8,128)(2,1)S(1)} %bitcast.51), channel_id=1, source_target_pairs={{2,0},{3,1},{4,2},{5,3},{6,4},{7,5},{8,6},{9,7},{10,8},{11,9},{12,... | collective-permute-start | bytes 393224 | tf_op jit(solution)/shard_map/ppermute | solution.py:12
  115.5 3.3 %collective-permute-start.14 = (bf16[8,128,64]{1,2,0:T(8,128)(2,1)S(1)}, bf16[8,128,64]{1,2,0:T(8,128)(2,1)S(1)}, u32[]{:S(2)}, u32[]{:S(2)}) collective-permute-start(bf16[8,128,64]{1,2,0:T(8,128)(2,1)S(1)} %bitcast.52), channel_id=1, source_target_pairs={{3,0},{4,1},{5,2},{6,3},{7,4},{8,5},{9,6},{10,7},{11,8},{12,9},{13... | collective-permute-start | bytes 393224 | tf_op jit(solution)/shard_map/ppermute | solution.py:12
  118.8 4.6 %collective-permute-start.15 = (bf16[8,128,64]{1,2,0:T(8,128)(2,1)S(1)}, bf16[8,128,64]{1,2,0:T(8,128)(2,1)S(1)}, u32[]{:S(2)}, u32[]{:S(2)}) collective-permute-start(bf16[8,128,64]{1,2,0:T(8,128)(2,1)S(1)} %bitcast.53), channel_id=1, source_target_pairs={{4,0},{5,1},{6,2},{7,3},{8,4},{9,5},{10,6},{11,7},{12,8},{13,9},{1... | collective-permute-start | bytes 393224 | tf_op jit(solution)/shard_map/ppermute | solution.py:12
  123.6 0.4 collective-permute-done.14
  124.0 5.5 %collective-permute-done.15 = bf16[8,128,64]{1,2,0:T(8,128)(2,1)S(1)} collective-permute-done((bf16[8,128,64]{1,2,0:T(8,128)(2,1)S(1)}, bf16[8,128,64]{1,2,0:T(8,128)(2,1)S(1)}, u32[]{:S(2)}, u32[]{:S(2)}) %collective-permute-start.15) | collective-permute-done | bytes 131104 | tf_op jit(solution)/shard_map/ppermute | solution.py:12
  129.6 0.7 gather_fusion.1
  130.3 3.0 %convolution_convert_fusion.1 = bf16[8,128,192]{1,2,0:T(8,128)(2,1)S(1)} fusion(bf16[8,192,192]{2,1,0:T(8,128)(2,1)} %param.10, bf16[8,192,8,64]{1,3,2,0:T(8,128)(2,1)} %bitcast.42, bf16[8,8,128,64]{2,3,1,0:T(8,128)(2,1)S(1)} %bitcast.41, pred[8,8]{1,0:T(8,128)(4,1)S(1)} %copy.30, pred[8,8]{1,0:T(8,128)(4,1)S(1)} %iota_compare_fusion, ...), kind=kOutput, calls=%fused_computation.14 | convolution fusion | flops 278659072 | bytes 3997824 | tf_op jit(solution)/shard_map/cnq,cqr->cnr/dot_general | solution.py:101
  133.4 0.5 convolution_convert_fusion
  133.8 0.3 copy.39
  134.1 4.6 %all_to_all.37 = bf16[8,128,256]{2,0,1:T(8,128)(2,1)S(1)} all-to-all(bf16[8,128,256]{2,0,1:T(8,128)(2,1)S(1)} %copy.39), channel_id=1, replica_groups=mesh['leaf'=128,'rhs'=2] {'rhs'}, dimensions={1} | all-to-all | bytes 1048576 | tf_op jit(solution)/shard_map/all_to_all | solution.py:107
  138.7 0.9 copy.40
  (44 shorter events, 0.7 us)
Async XLA Ops:
  0.0 5.7 %copy-start = (bf16[8,256,256]{2,1,0:T(8,128)(2,1)S(1)}, bf16[8,256,256]{2,1,0:T(8,128)(2,1)}, u32[]{:S(2)}) copy-start(bf16[8,256,256]{2,1,0:T(8,128)(2,1)} %param.9) | copy-start | bytes 3145732
  5.7 1.1 copy-start.3
  5.7 20.0 %copy-start.5 = (s32[16,8]{0,1:T(8,128)S(1)}, s32[16,8]{0,1:T(8,128)}, u32[]{:S(2)}) copy-start(s32[16,8]{0,1:T(8,128)} %param.14) | copy-start | bytes 1540
  5.7 20.3 %copy-start.6 = (s32[16]{0:T(128)S(1)}, s32[16]{0:T(128)}, u32[]{:S(2)}) copy-start(s32[16]{0:T(128)} %param.15) | copy-start | bytes 196
  7.2 55.1 %copy-start.2 = (bf16[8,128,192]{1,2,0:T(8,128)(2,1)}, bf16[8,128,192]{1,2,0:T(8,128)(2,1)S(1)}, u32[]{:S(2)}) copy-start(bf16[8,128,192]{1,2,0:T(8,128)(2,1)S(1)} %convolution_convert_fusion.2) | copy-start | bytes 1179652
  7.2 23.4 %collective-permute-start = (bf16[8,128,192]{1,2,0:T(8,128)(2,1)S(1)}, bf16[8,128,192]{1,2,0:T(8,128)(2,1)}, u32[]{:S(2)}, u32[]{:S(2)}) collective-permute-start(bf16[8,128,192]{1,2,0:T(8,128)(2,1)S(1)} %convolution_convert_fusion.2), channel_id=1, source_target_pairs={{0,4},{1,5},{2,6},{3,7},{4,8},{5,9},{6,10},{7,11},{8,12},{9,13},{1... | collective-permute-start | bytes 1179656 | tf_op jit(solution)/shard_map/ppermute | solution.py:12
  12.1 35.7 %collective-permute-start.1 = (bf16[8,128,192]{1,2,0:T(8,128)(2,1)S(1)}, bf16[8,128,192]{1,2,0:T(8,128)(2,1)}, u32[]{:S(2)}, u32[]{:S(2)}) collective-permute-start(bf16[8,128,192]{1,2,0:T(8,128)(2,1)S(1)} %convolution_convert_fusion.2), channel_id=1, source_target_pairs={{0,3},{1,4},{2,5},{3,6},{4,7},{5,8},{6,9},{7,10},{8,11},{9,12},{10... | collective-permute-start | bytes 1179656 | tf_op jit(solution)/shard_map/ppermute | solution.py:12
  18.7 36.7 %collective-permute-start.2 = (bf16[8,128,192]{1,2,0:T(8,128)(2,1)S(1)}, bf16[8,128,192]{1,2,0:T(8,128)(2,1)}, u32[]{:S(2)}, u32[]{:S(2)}) collective-permute-start(bf16[8,128,192]{1,2,0:T(8,128)(2,1)S(1)} %convolution_convert_fusion.2), channel_id=1, source_target_pairs={{0,2},{1,3},{2,4},{3,5},{4,6},{5,7},{6,8},{7,9},{8,10},{9,11},{10,... | collective-permute-start | bytes 1179656 | tf_op jit(solution)/shard_map/ppermute | solution.py:12
  21.4 40.1 %collective-permute-start.3 = (bf16[8,128,192]{1,2,0:T(8,128)(2,1)S(1)}, bf16[8,128,192]{1,2,0:T(8,128)(2,1)S(1)}, u32[]{:S(2)}, u32[]{:S(2)}) collective-permute-start(bf16[8,128,192]{1,2,0:T(8,128)(2,1)S(1)} %convolution_convert_fusion.2), channel_id=1, source_target_pairs={{0,1},{1,2},{2,3},{3,4},{4,5},{5,6},{6,7},{7,8},{8,9},{9,10},{10,1... | collective-permute-start | bytes 1179656 | tf_op jit(solution)/shard_map/ppermute | solution.py:12
  23.6 39.5 %collective-permute-start.4 = (bf16[8,128,192]{1,2,0:T(8,128)(2,1)S(1)}, bf16[8,128,192]{1,2,0:T(8,128)(2,1)S(1)}, u32[]{:S(2)}, u32[]{:S(2)}) collective-permute-start(bf16[8,128,192]{1,2,0:T(8,128)(2,1)S(1)} %convolution_convert_fusion.2), channel_id=1, source_target_pairs={{1,0},{2,1},{3,2},{4,3},{5,4},{6,5},{7,6},{8,7},{9,8},{10,9},{11,1... | collective-permute-start | bytes 1179656 | tf_op jit(solution)/shard_map/ppermute | solution.py:12
  30.6 33.3 %collective-permute-start.5 = (bf16[8,128,192]{1,2,0:T(8,128)(2,1)S(1)}, bf16[8,128,192]{1,2,0:T(8,128)(2,1)S(1)}, u32[]{:S(2)}, u32[]{:S(2)}) collective-permute-start(bf16[8,128,192]{1,2,0:T(8,128)(2,1)S(1)} %convolution_convert_fusion.2), channel_id=1, source_target_pairs={{2,0},{3,1},{4,2},{5,3},{6,4},{7,5},{8,6},{9,7},{10,8},{11,9},{12,... | collective-permute-start | bytes 1179656 | tf_op jit(solution)/shard_map/ppermute | solution.py:12
  47.8 25.0 %collective-permute-start.6 = (bf16[8,128,192]{1,2,0:T(8,128)(2,1)S(1)}, bf16[8,128,192]{1,2,0:T(8,128)(2,1)S(1)}, u32[]{:S(2)}, u32[]{:S(2)}) collective-permute-start(bf16[8,128,192]{1,2,0:T(8,128)(2,1)S(1)} %convolution_convert_fusion.2), channel_id=1, source_target_pairs={{3,0},{4,1},{5,2},{6,3},{7,4},{8,5},{9,6},{10,7},{11,8},{12,9},{13... | collective-permute-start | bytes 1179656 | tf_op jit(solution)/shard_map/ppermute | solution.py:12
  55.4 25.2 %collective-permute-start.7 = (bf16[8,128,192]{1,2,0:T(8,128)(2,1)S(1)}, bf16[8,128,192]{1,2,0:T(8,128)(2,1)S(1)}, u32[]{:S(2)}, u32[]{:S(2)}) collective-permute-start(bf16[8,128,192]{1,2,0:T(8,128)(2,1)S(1)} %convolution_convert_fusion.2), channel_id=1, source_target_pairs={{4,0},{5,1},{6,2},{7,3},{8,4},{9,5},{10,6},{11,7},{12,8},{13,9},{1... | collective-permute-start | bytes 1179656 | tf_op jit(solution)/shard_map/ppermute | solution.py:12
  86.0 4.4 %copy-start.4 = (bf16[4,128,128]{2,1,0:T(8,128)(2,1)S(1)}, bf16[4,128,128]{2,1,0:T(8,128)(2,1)}, u32[]{:S(2)}) copy-start(bf16[4,128,128]{2,1,0:T(8,128)(2,1)} %param.13) | copy-start | bytes 393220
  90.4 8.8 %copy-start.1 = (bf16[8,192,512]{2,1,0:T(8,128)(2,1)S(1)}, bf16[8,192,512]{2,1,0:T(8,128)(2,1)}, u32[]{:S(2)}) copy-start(bf16[8,192,512]{2,1,0:T(8,128)(2,1)} %param.12) | copy-start | bytes 4718596
  90.8 17.2 %collective-permute-start.8 = (bf16[8,128,64]{1,2,0:T(8,128)(2,1)S(1)}, bf16[8,128,64]{1,2,0:T(8,128)(2,1)S(1)}, u32[]{:S(2)}, u32[]{:S(2)}) collective-permute-start(bf16[8,128,64]{1,2,0:T(8,128)(2,1)S(1)} %bitcast.46), channel_id=1, source_target_pairs={{0,4},{1,5},{2,6},{3,7},{4,8},{5,9},{6,10},{7,11},{8,12},{9,13},{1... | collective-permute-start | bytes 393224 | tf_op jit(solution)/shard_map/ppermute | solution.py:12
  95.1 20.4 %collective-permute-start.9 = (bf16[8,128,64]{1,2,0:T(8,128)(2,1)S(1)}, bf16[8,128,64]{1,2,0:T(8,128)(2,1)S(1)}, u32[]{:S(2)}, u32[]{:S(2)}) collective-permute-start(bf16[8,128,64]{1,2,0:T(8,128)(2,1)S(1)} %bitcast.47), channel_id=1, source_target_pairs={{0,3},{1,4},{2,5},{3,6},{4,7},{5,8},{6,9},{7,10},{8,11},{9,12},{10... | collective-permute-start | bytes 393224 | tf_op jit(solution)/shard_map/ppermute | solution.py:12
  101.6 17.2 %collective-permute-start.10 = (bf16[8,128,64]{1,2,0:T(8,128)(2,1)S(1)}, bf16[8,128,64]{1,2,0:T(8,128)(2,1)S(1)}, u32[]{:S(2)}, u32[]{:S(2)}) collective-permute-start(bf16[8,128,64]{1,2,0:T(8,128)(2,1)S(1)} %bitcast.48), channel_id=1, source_target_pairs={{0,2},{1,3},{2,4},{3,5},{4,6},{5,7},{6,8},{7,9},{8,10},{9,11},{10,... | collective-permute-start | bytes 393224 | tf_op jit(solution)/shard_map/ppermute | solution.py:12
  103.5 19.9 %collective-permute-start.11 = (bf16[8,128,64]{1,2,0:T(8,128)(2,1)S(1)}, bf16[8,128,64]{1,2,0:T(8,128)(2,1)S(1)}, u32[]{:S(2)}, u32[]{:S(2)}) collective-permute-start(bf16[8,128,64]{1,2,0:T(8,128)(2,1)S(1)} %bitcast.49), channel_id=1, source_target_pairs={{0,1},{1,2},{2,3},{3,4},{4,5},{5,6},{6,7},{7,8},{8,9},{9,10},{10,1... | collective-permute-start | bytes 393224 | tf_op jit(solution)/shard_map/ppermute | solution.py:12
  106.0 17.5 %collective-permute-start.12 = (bf16[8,128,64]{1,2,0:T(8,128)(2,1)S(1)}, bf16[8,128,64]{1,2,0:T(8,128)(2,1)S(1)}, u32[]{:S(2)}, u32[]{:S(2)}) collective-permute-start(bf16[8,128,64]{1,2,0:T(8,128)(2,1)S(1)} %bitcast.50), channel_id=1, source_target_pairs={{1,0},{2,1},{3,2},{4,3},{5,4},{6,5},{7,6},{8,7},{9,8},{10,9},{11,1... | collective-permute-start | bytes 393224 | tf_op jit(solution)/shard_map/ppermute | solution.py:12
  108.0 15.6 %collective-permute-start.13 = (bf16[8,128,64]{1,2,0:T(8,128)(2,1)S(1)}, bf16[8,128,64]{1,2,0:T(8,128)(2,1)S(1)}, u32[]{:S(2)}, u32[]{:S(2)}) collective-permute-start(bf16[8,128,64]{1,2,0:T(8,128)(2,1)S(1)} %bitcast.51), channel_id=1, source_target_pairs={{2,0},{3,1},{4,2},{5,3},{6,4},{7,5},{8,6},{9,7},{10,8},{11,9},{12,... | collective-permute-start | bytes 393224 | tf_op jit(solution)/shard_map/ppermute | solution.py:12
  115.5 8.5 %collective-permute-start.14 = (bf16[8,128,64]{1,2,0:T(8,128)(2,1)S(1)}, bf16[8,128,64]{1,2,0:T(8,128)(2,1)S(1)}, u32[]{:S(2)}, u32[]{:S(2)}) collective-permute-start(bf16[8,128,64]{1,2,0:T(8,128)(2,1)S(1)} %bitcast.52), channel_id=1, source_target_pairs={{3,0},{4,1},{5,2},{6,3},{7,4},{8,5},{9,6},{10,7},{11,8},{12,9},{13... | collective-permute-start | bytes 393224 | tf_op jit(solution)/shard_map/ppermute | solution.py:12
  118.8 10.7 %collective-permute-start.15 = (bf16[8,128,64]{1,2,0:T(8,128)(2,1)S(1)}, bf16[8,128,64]{1,2,0:T(8,128)(2,1)S(1)}, u32[]{:S(2)}, u32[]{:S(2)}) collective-permute-start(bf16[8,128,64]{1,2,0:T(8,128)(2,1)S(1)} %bitcast.53), channel_id=1, source_target_pairs={{4,0},{5,1},{6,2},{7,3},{8,4},{9,5},{10,6},{11,7},{12,8},{13,9},{1... | collective-permute-start | bytes 393224 | tf_op jit(solution)/shard_map/ppermute | solution.py:12
where the time goes:
time: 141 us; the launch traced here: 140 us
  starting transfers between devices  65.9 us (47%)
  waiting for transfers between devices  29.4 us (21%)
  local copies, waits for them, and re-layouts  24.6 us (17%)
  blocking collectives  10.2 us (7%)
  matrix products  8.82 us (6%)
    ppermute x16, starting transfers between devices, passed_along(): lax.ppermute(value, axis, [(source, source + steps) for source in range(l...  65.9 us
    ppermute x16, waiting for transfers between devices, passed_along(): lax.ppermute(value, axis, [(source, source + steps) for source in range(l...  29.4 us
    unnamed x31, local copies, waits for them, and re-layouts  12.6 us
    all_to_all x1, blocking collectives, on_device(): lax.all_to_all(rhs_block, 'rhs', split_axis=0, concat_axis=1, tiled=True)  5.65 us
    gather x2, local copies, waits for them, and re-layouts, collect(): picked = jnp.take(window, indices.reshape(-1), axis=0)  5.37 us
    all_to_all x1, blocking collectives, on_device(): lax.all_to_all(solution, 'rhs', split_axis=1, concat_axis=0, tiled=True)  4.58 us
    dot_general x1, matrix products, on_device(): jnp.einsum('ckna,cqka->cnq', near_redundant, forward_blocks, preferred_el...  4.34 us
    reshape x1, local copies, waits for them, and re-layouts, on_device(): forward_all.reshape(owned_rows, skeleton, slot_count, redundant_rows)  4.26 us
  transfers between devices with their start and end apart: 16, of which 6 were waited for; matrix products, arithmetic and copies ran while one was open for 12% of the time, Pallas kernels for 0%

commit v1 on v0

v1 whole, which is shorter than its diff:
```python
import functools

import jax
import jax.numpy as jnp
from jax import lax
from jax.experimental import pallas as pl
from jax.experimental.pallas import tpu as pltpu
from jax.sharding import PartitionSpec as P


HALF = 64
ROWS = 40
F32 = jnp.float32
BF16 = jnp.bfloat16
NT = (((1,), (1,)), ((), ()))
SMEM = pl.BlockSpec(memory_space=pltpu.SMEM)
VMEM = pl.BlockSpec(memory_space=pltpu.VMEM)
HBM = pl.BlockSpec(memory_space=pltpu.HBM)


def shape(*dims, dtype=BF16):
    return jax.ShapeDtypeStruct(dims, dtype)


def cost(flops, moved):
    return pl.CostEstimate(flops=flops, bytes_accessed=moved, transcendentals=0)


def limit(mebibytes):
    return pltpu.CompilerParams(vmem_limit_bytes=mebibytes << 20)


def in_hbm(*values):
    return [pltpu.with_memory_space_constraint(value, pltpu.HBM) for value in values]


def both_ways(pairs):
    return [(a, b) for a, b in pairs] + [(b, a) for a, b in pairs]


def leaf_pairs(count):
    inner = both_ways([(i, i + 1) for i in range(0, count - 1, 2)])
    outer = both_ways([(i, i + 1) for i in range(1, count - 1, 2)])
    near = both_ways([(i, i + 2) for i in range(count - 2) if i % 4 in (0, 1)])
    far = both_ways([(i, i + 2) for i in range(count - 2) if i % 4 in (2, 3)])
    return inner, outer, near, far


def swap(value):
    return lax.ppermute(value, "rhs", [(0, 1), (1, 0)])


def along(value, pairs):
    return lax.ppermute(value, "leaf", pairs)


def low_lanes():
    return lax.broadcasted_iota(jnp.int32, (1, 2 * HALF), 1) < HALF


def turned(value):
    return pltpu.roll(value, HALF, 1)


def tables_kernel(near_ref, count_ref, forward_ref, backward_ref):
    leaf, core = lax.axis_index("leaf"), lax.axis_index("rhs")
    sign = 1 - 2 * (leaf & 1)
    flip = jnp.where((leaf & 3 == 1) | (leaf & 3 == 2), 7, 0)
    target = near_ref[...]
    slot = lax.broadcasted_iota(jnp.int32, target.shape, 0)
    cluster = lax.broadcasted_iota(jnp.int32, target.shape, 1)
    used = slot < count_ref[...]
    away = (lax.shift_right_logical(target, 4) - leaf) * sign
    block = jnp.where(away > 0, 2 * away - 1, -2 * away)
    other = jnp.where(block >= 3, block ^ flip, block)
    inside = target & 15
    place = lax.shift_right_logical(inside ^ (core << 3), 1)
    side = inside & 1
    forward = block * 8 + place + (side ^ (lax.shift_right_logical(cluster, 1) & 1)) * ROWS
    backward = other * 8 + place + (side ^ (slot & 1)) * ROWS
    forward_ref[...] = jnp.where(used, forward, 2 * ROWS)
    backward_ref[...] = jnp.where(used, backward, 2 * ROWS)


def tables(near_index, near_count):
    slots = near_index.T
    return pl.pallas_call(
        tables_kernel,
        out_shape=[shape(*slots.shape, dtype=jnp.int32)] * 2,
        in_specs=[VMEM] * 2,
        out_specs=[VMEM] * 2,
        name="tables",
        cost_estimate=cost(10000, 10000),
        compiler_params=limit(1),
    )(slots, near_count.reshape(1, -1))


def project_pair(pair, base, rhs_ref, basis_ref, inverse_ref, elim_ref, skel_ref):
    redundant = inverse_ref.shape[1]
    zeros = jnp.zeros((HALF, redundant), BF16)
    elim = None
    tails = []
    for t in range(2):
        j = 2 * pair + t
        projected = jnp.dot(rhs_ref[base + j], basis_ref[j], preferred_element_type=F32)
        head = projected[:, :redundant].astype(BF16)
        tails.append(projected[:, 128:])
        stack = [head, zeros] if t == 0 else [zeros, head]
        part = lax.dot_general(
            inverse_ref[j], jnp.concatenate(stack, axis=0), NT, preferred_element_type=F32
        )
        elim = part if elim is None else elim + part
    elim_ref[pair] = elim.astype(BF16)
    skel_ref[pair] = jnp.concatenate(tails, axis=0).T[HALF:, :]


def project_own_kernel(
    rhs_hbm, basis_hbm, inverse_hbm, elim_ref, skel_ref, rest_ref, basis, inverse, rhs, sems, rest_sem
):
    core = lax.axis_index("rhs")
    base = core * 8
    copies = []
    for pair in range(4):
        here = pl.ds(2 * pair, 2)
        group = [
            pltpu.make_async_copy(rhs_hbm.at[pl.ds(base + 2 * pair, 2)], rhs.at[here], sems.at[pair, 0]),
            pltpu.make_async_copy(basis_hbm.at[here], basis.at[here], sems.at[pair, 1]),
            pltpu.make_async_copy(inverse_hbm.at[here], inverse.at[here], sems.at[pair, 2]),
        ]
        for copy in group:
            copy.start()
        copies.append(group)
    rest = pltpu.make_async_copy(rhs_hbm.at[pl.ds(8 - base, 8)], rest_ref, rest_sem)
    rest.start()
    for group in copies:
        for copy in group:
            copy.wait()
    for pair in range(4):
        project_pair(pair, 0, rhs, basis, inverse, elim_ref, skel_ref)
    rest.wait()


def project_own(rhs_block, basis, inverse):
    return pl.pallas_call(
        project_own_kernel,
        out_shape=[
            shape(4, 192, 128),
            shape(4, 64, 128, dtype=F32),
            shape(8, *rhs_block.shape[1:]),
            shape(*basis.shape),
            shape(*inverse.shape),
        ],
        in_specs=[HBM] * 3,
        out_specs=[VMEM] * 5,
        scratch_shapes=[
            pltpu.VMEM((8,) + rhs_block.shape[1:], BF16),
            pltpu.SemaphoreType.DMA((4, 3)),
            pltpu.SemaphoreType.DMA(()),
        ],
        name="project_own",
        cost_estimate=cost(2 * 8 * 64 * (65536 + 36864), 2500000),
        compiler_params=limit(8),
    )(*in_hbm(rhs_block, basis, inverse))


def project_other_kernel(rhs_ref, basis_ref, inverse_ref, elim_ref, skel_ref):
    for pair in range(4):
        project_pair(pair, 0, rhs_ref, basis_ref, inverse_ref, elim_ref, skel_ref)


def project_other(rhs_block, basis, inverse):
    return pl.pallas_call(
        project_other_kernel,
        out_shape=[shape(4, 192, 128), shape(4, 64, 128, dtype=F32)],
        in_specs=[VMEM] * 3,
        out_specs=[VMEM] * 2,
        name="project_other",
        cost_estimate=cost(2 * 8 * 64 * (65536 + 36864), 2500000),
        compiler_params=limit(6),
    )(rhs_block, basis, inverse)


def place_block(window, block, first):
    for pair in range(block.shape[0]):
        value = block[pair]
        window[first + pair] = value
        window[first + pair + ROWS] = turned(value)


def gather_kernel(firsts, fresh, *refs):
    window = refs[-1]
    blocks = refs[:-1] if fresh else refs[1:-1]
    for first, block in zip(firsts, blocks):
        place_block(window, block, first)
    if fresh:
        window[2 * ROWS] = jnp.zeros(window.shape[1:], BF16)


def gather(firsts, blocks, window=None):
    fresh = window is None
    operands = blocks if fresh else (window,) + blocks
    return pl.pallas_call(
        functools.partial(gather_kernel, firsts, fresh),
        out_shape=shape(2 * ROWS + 1, 192, 128),
        in_specs=[VMEM] * len(operands),
        out_specs=VMEM,
        input_output_aliases={} if fresh else {0: 0},
        name="gather",
        cost_estimate=cost(1000, 4000000),
        compiler_params=limit(6),
    )(*operands)


def fold_kernel(elim_ref, inverse_ref, basis_ref, backward_ref, wide_ref, base_ref, tail_ref):
    redundant = inverse_ref.shape[1]
    for pair in range(4):
        elim = elim_ref[pair].astype(F32).T.astype(BF16)
        for t in range(2):
            j = 2 * pair + t
            both = lax.dot_general(
                basis_ref[j][:, :redundant], inverse_ref[j], NT, preferred_element_type=F32
            ).astype(BF16)
            wide_ref[j] = jnp.dot(both, backward_ref[j], preferred_element_type=F32).astype(BF16)
            base_ref[j] = lax.dot_general(
                elim[t * HALF : (t + 1) * HALF, :], both, NT, preferred_element_type=F32
            )
            tail_ref[j] = basis_ref[j][:, 128:]


def fold(elim, inverse, basis, backward):
    return pl.pallas_call(
        fold_kernel,
        out_shape=(shape(8, 256, 512), shape(8, 64, 256, dtype=F32), shape(8, 256, 128)),
        in_specs=[VMEM] * 4,
        out_specs=[VMEM] * 3,
        name="fold",
        cost_estimate=cost(2 * 8 * 256 * 192 * 768, 8000000),
        compiler_params=limit(6),
    )(elim, inverse, basis, backward)


def reduce_kernel(table_ref, window_in, *refs):
    blocks = refs[:2]
    f_refs = refs[2:4]
    skel_refs = refs[4:6]
    parent_refs = refs[6:8]
    out_ref, window = refs[8:]
    core = lax.axis_index("rhs")
    for first, block in zip((28, 36), blocks):
        place_block(window, block, first)
    low = low_lanes()
    for h in range(2):
        for two in range(2):
            solved = []
            for parity in range(2):
                pair = 2 * two + parity
                skel = skel_refs[h][pair]
                reduced = []
                for t in range(2):
                    j = 2 * pair + t
                    parts = [window[table_ref[k, (core ^ h) * 8 + j]] for k in range(8)]
                    total = jnp.dot(
                        f_refs[h][j], jnp.concatenate(parts, axis=0), preferred_element_type=F32
                    )
                    reduced.append(((skel if t == parity else turned(skel)) - total).astype(BF16))
                solved.append(
                    jnp.dot(
                        parent_refs[h][pair], jnp.concatenate(reduced, axis=0), preferred_element_type=F32
                    )
                )
            both = jnp.where(low, solved[0], solved[1]).T.astype(BF16)
            for parity in range(2):
                out_ref[4 * h + 2 * two + parity] = both[parity * HALF : (parity + 1) * HALF, :]


def reduce_and_solve(table, window, blocks, forward, skel, parent):
    return pl.pallas_call(
        reduce_kernel,
        out_shape=(shape(8, 64, 128), shape(*window.shape)),
        in_specs=[SMEM] + [VMEM] * 9,
        out_specs=[VMEM] * 2,
        input_output_aliases={1: 1},
        name="reduce_and_solve",
        cost_estimate=cost(2 * 16 * 64 * 1536 * 128, 6000000),
        compiler_params=limit(6),
    )(table, window, *blocks, *forward, *skel, *parent)[0]


def own_kernel(own_ref, *refs):
    tail_refs, base_refs, out_ref = refs[:2], refs[2:4], refs[4]
    low = low_lanes()
    for h in range(2):
        for pair in range(4):
            own = own_ref[4 * h + pair].astype(F32)
            for t in range(2):
                j = 2 * pair + t
                tail = jnp.where(low, 0.0, turned(own) if t == 0 else own).astype(BF16)
                out_ref[8 * h + j] = base_refs[h][j] + lax.dot_general(
                    tail, tail_refs[h][j], NT, preferred_element_type=F32
                )


def add_own(own, tails, base):
    return pl.pallas_call(
        own_kernel,
        out_shape=shape(16, 64, 256, dtype=F32),
        in_specs=[VMEM] * 5,
        out_specs=VMEM,
        name="add_own",
        cost_estimate=cost(2 * 16 * 64 * 128 * 256, 4000000),
        compiler_params=limit(4),
    )(own, *tails, *base)


def finish_kernel(table_ref, *refs):
    blocks, wide_refs, base_ref, out_ref, window = refs[:5], refs[5:7], refs[7], refs[8], refs[9]
    for n, block in enumerate(blocks):
        place_block(window, block, 8 * n)
    window[2 * ROWS] = jnp.zeros(window.shape[1:], BF16)
    core = lax.axis_index("rhs")
    low = low_lanes()
    for h in range(2):
        for j in range(8):
            cluster = (core ^ h) * 8 + j
            parts = []
            for k in range(0, 8, 2):
                left, right = window[table_ref[k, cluster]], window[table_ref[k + 1, cluster]]
                parts.append(jnp.where(low, left, right))
            carried = lax.dot_general(
                jnp.concatenate(parts, axis=1), wide_refs[h][j], NT, preferred_element_type=F32
            )
            out_ref[cluster] = (base_ref[8 * h + j] - carried).astype(BF16)


def finish(table, blocks, wide, base):
    return pl.pallas_call(
        finish_kernel,
        out_shape=shape(16, 64, 256),
        in_specs=[SMEM] + [VMEM] * 8,
        out_specs=VMEM,
        scratch_shapes=[pltpu.VMEM((2 * ROWS + 1, 64, 128), BF16)],
        name="finish",
        cost_estimate=cost(2 * 16 * 64 * 512 * 256, 6000000),
        compiler_params=limit(6),
    )(table, *blocks, *wide, base)


def on_device(
    rhs_block,
    basis,
    red_inverse,
    forward_coupling,
    backward_coupling,
    parent_inverse,
    near_index,
    near_count,
):
    inner, outer, near, far = leaf_pairs(lax.axis_size("leaf"))
    basis_b = swap(basis)
    inverse_b = swap(red_inverse)
    elim_a, skel_a, rest, basis_a, inverse_a = project_own(rhs_block, basis, red_inverse)
    inner_a = along(elim_a, inner)
    outer_a = along(elim_a, outer)
    elim_b, skel_b = project_other(rest, basis_b, inverse_b)
    inner_b = along(elim_b, inner)
    outer_b = along(elim_b, outer)
    parent_b = swap(parent_inverse)
    forward_b = swap(forward_coupling)
    backward_b = swap(backward_coupling)
    far_outer_a = along(inner_a, outer)
    far_inner_a = along(outer_a, inner)
    far_outer_b = along(inner_b, outer)
    far_inner_b = along(outer_b, inner)
    forward_table, backward_table = tables(near_index, near_count)
    window_blocks = (elim_a, elim_b, inner_a, inner_b, outer_a, outer_b)
    window = gather((0, 4, 8, 12, 16, 20), window_blocks)
    window = gather((24, 32), (far_inner_a, far_outer_a), window)
    wide_a, base_a, tail_a = fold(elim_a, inverse_a, basis_a, backward_coupling)
    wide_b, base_b, tail_b = fold(elim_b, inverse_b, basis_b, backward_b)
    factors = (forward_coupling, forward_b), (skel_a, skel_b), (parent_inverse, parent_b)
    skeleton = reduce_and_solve(forward_table, window, (far_inner_b, far_outer_b), *factors)
    near_s = along(skeleton, near)
    inner_s = along(skeleton, inner)
    far_s = along(skeleton, far)
    outer_s = along(skeleton, outer)
    base = add_own(skeleton, (tail_a, tail_b), (base_a, base_b))
    return finish(backward_table, (skeleton, inner_s, outer_s, near_s, far_s), (wide_a, wide_b), base)


def solution(mesh):
    whole = P(("leaf", "rhs"), None, None)
    in_specs = (P("leaf", "rhs", None), whole, whole, whole, whole, whole, P("leaf", None), P("leaf"))
    return jax.shard_map(
        on_device, mesh=mesh, in_specs=in_specs, out_specs=P("leaf", "rhs", None), check_vma=False
    )
```

time: 141 us -> 75.5 us (0.54)
  local copies, waits for them, and re-layouts: 24.6 us -> 0.5 us
  starting transfers between devices: 65.9 us -> 47.7 us
  waiting for transfers between devices: 29.4 us -> 11.5 us
  Pallas kernels: 0 us -> 14.9 us
  blocking collectives: 10.2 us -> 0 us
  matrix products: 8.82 us -> 0 us
    ppermute x16 -> x17, starting transfers between devices: 65.9 us -> 47.7 us  [the longest x12 41.4 us: along(): return lax.ppermute(value, 'leaf', pairs)]
    ppermute x16 -> x17, waiting for transfers between devices: 29.4 us -> 11.5 us  [the longest x12 11.3 us: along(): return lax.ppermute(value, 'leaf', pairs)]
    pallas_call x0 -> x10, Pallas kernels: none -> 14.9 us  [the longest x2 4.45 us: fold(): pl.pallas_call(fold_kernel, out_shape=(shape(8, 256, 512), shape(8, 64, 2...]
    unnamed x31 -> x10, local copies, waits for them, and re-layouts: 12.6 us -> 0.5 us
    all_to_all x2 -> x0, blocking collectives: 10.2 us -> none  [the longest x1 5.65 us: on_device(): lax.all_to_all(rhs_block, 'rhs', split_axis=0, concat_axis=1, tiled=True)]
    dot_general x6 -> x0, matrix products: 8.82 us -> none  [the longest x1 4.34 us: on_device(): jnp.einsum('ckna,cqka->cnq', near_redundant, forward_blocks, preferred_el...]
    gather x2 -> x0, local copies, waits for them, and re-layouts: 5.37 us -> none  [collect(): picked = jnp.take(window, indices.reshape(-1), axis=0)]
    reshape x2 -> x0, local copies, waits for them, and re-layouts: 4.34 us -> none  [the longest x1 4.26 us: on_device(): forward_all.reshape(owned_rows, skeleton, slot_count, redundant_rows)]
  transfers between devices with their start and end apart: 16 -> 17, of which waited for: 6 -> 4; matrix products, arithmetic and copies ran while one was open for 12% -> 0% of each run, Pallas kernels for 0% -> 16%
where the time goes in v1:
time: 75.5 us; the launch traced here: 74.9 us
  starting transfers between devices  47.7 us (63%)
  Pallas kernels  14.9 us (20%)
  waiting for transfers between devices  11.5 us (15%)
    ppermute x12, starting transfers between devices, along(): return lax.ppermute(value, 'leaf', pairs)  41.4 us
    ppermute x12, waiting for transfers between devices, along(): return lax.ppermute(value, 'leaf', pairs)  11.3 us
    ppermute x5, starting transfers between devices, swap(): return lax.ppermute(value, 'rhs', [(0, 1), (1, 0)])  6.35 us
    pallas_call x2, Pallas kernels, fold(): pl.pallas_call(fold_kernel, out_shape=(shape(8, 256, 512), shape(8, 64, 2...  4.45 us
    pallas_call x1, Pallas kernels, finish(): pl.pallas_call(finish_kernel, out_shape=shape(16, 64, 256), in_specs=[SME...  3.05 us
    pallas_call x1, Pallas kernels, reduce_and_solve(): pl.pallas_call(reduce_kernel, out_shape=(shape(8, 64, 128), shape(*window...  2.99 us
    pallas_call x1, Pallas kernels, project_own(): pl.pallas_call(project_own_kernel, out_shape=[shape(4, 192, 128), shape(4...  2.4 us
  transfers between devices with their start and end apart: 17, of which 4 were waited for; matrix products, arithmetic and copies ran while one was open for 0% of the time, Pallas kernels for 16%

profile of v1, /device:TPU:9, one launch (start us, length us, event | category | flops | bytes accessed | tf_op | source)
XLA Modules:
  0.0 74.9 jit_solution(18188170211817241789)
XLA Ops:
  0.0 0.7 collective-permute-start.10
  0.7 0.1 collective-permute-start.16
  0.8 0.4 collective-permute-start
  1.2 0.1 collective-permute-start.1
  1.3 2.4 %project_own.1 = (bf16[4,192,128]{2,1,0:T(8,128)(2,1)S(1)}, f32[4,64,128]{2,1,0:T(8,128)S(1)}, bf16[8,64,256]{2,1,0:T(8,128)(2,1)S(1)}, bf16[8,256,256]{2,1,0:T(8,128)(2,1)S(1)}, bf16[8,192,192]{2,1,0:T(8,128)(2,1)S(1)}) custom-call(bf16[16,64,256]{2,1,0:T(8,128)(2,1)} %rhs_hbm.1, bf16[8,256,256]{2,1,0:T(8,128)(2,1)} %basis_hbm.1, ...), custom_call_target="tpu_custom_call" | custom-call | flops 104857600 | bytes 2500000 | tf_op jit(solution)/shard_map/project_own/pallas_call | solution.py:144
  3.7 9.6 %collective-permute-start.4 = (bf16[4,192,128]{2,1,0:T(8,128)(2,1)S(1)}, bf16[4,192,128]{2,1,0:T(8,128)(2,1)S(1)}, u32[]{:S(2)}, u32[]{:S(2)}) collective-permute-start(bf16[4,192,128]{2,1,0:T(8,128)(2,1)S(1)} %get-tuple-element.23.refs_0_.elim_ref), channel_id=1, source_target_pairs={{2,4},{6,8},{10,12},{14,16},{18,20},{22,24},{26,28},{30,32},{34,36... | collective-permute-start | bytes 589832 | tf_op jit(solution)/shard_map/ppermute | solution.py:54
  13.3 4.8 %collective-permute-done.4.refs_4_ = bf16[4,192,128]{2,1,0:T(8,128)(2,1)S(1)} collective-permute-done((bf16[4,192,128]{2,1,0:T(8,128)(2,1)S(1)}, bf16[4,192,128]{2,1,0:T(8,128)(2,1)S(1)}, u32[]{:S(2)}, u32[]{:S(2)}) %collective-permute-start.4) | collective-permute-done | bytes 196640 | tf_op jit(solution)/shard_map/ppermute | solution.py:54
  18.1 0.0 collective-permute-start.2
  18.1 0.0 collective-permute-done.1.inverse_ref
  18.1 1.5 %collective-permute-start.6 = (bf16[4,192,128]{2,1,0:T(8,128)(2,1)S(1)}, bf16[4,192,128]{2,1,0:T(8,128)(2,1)S(1)}, u32[]{:S(2)}, u32[]{:S(2)}) collective-permute-start(bf16[4,192,128]{2,1,0:T(8,128)(2,1)S(1)} %collective-permute-done.4.refs_4_), channel_id=1, source_target_pairs={{0,2},{4,6},{8,10},{12,14},{16,18},{20,22},{24,26},{28,30},{32,34}... | collective-permute-start | bytes 589832 | tf_op jit(solution)/shard_map/ppermute | solution.py:54
  19.6 0.0 collective-permute-done.basis_ref
  19.6 0.7 project_other.1
  20.3 0.0 copy-start.3
  20.3 0.0 copy-start.4
  20.4 7.3 %collective-permute-start.5 = (bf16[4,192,128]{2,1,0:T(8,128)(2,1)S(1)}, bf16[4,192,128]{2,1,0:T(8,128)(2,1)S(1)}, u32[]{:S(2)}, u32[]{:S(2)}) collective-permute-start(bf16[4,192,128]{2,1,0:T(8,128)(2,1)S(1)} %get-tuple-element.25.refs_1_.elim_ref), channel_id=1, source_target_pairs={{2,4},{6,8},{10,12},{14,16},{18,20},{22,24},{26,28},{30,32},{34,36... | collective-permute-start | bytes 589832 | tf_op jit(solution)/shard_map/ppermute | solution.py:54
  27.7 0.0 collective-permute-done.2.refs_2_
  27.7 0.1 collective-permute-start.3
  27.8 0.0 collective-permute-done.6.refs_1_
  27.8 7.0 %collective-permute-start.7 = (bf16[4,192,128]{2,1,0:T(8,128)(2,1)S(1)}, bf16[4,192,128]{2,1,0:T(8,128)(2,1)S(1)}, u32[]{:S(2)}, u32[]{:S(2)}) collective-permute-start(bf16[4,192,128]{2,1,0:T(8,128)(2,1)S(1)} %collective-permute-done.2.refs_2_), channel_id=1, source_target_pairs={{2,4},{6,8},{10,12},{14,16},{18,20},{22,24},{26,28},{30,32},{34,36... | collective-permute-start | bytes 589832 | tf_op jit(solution)/shard_map/ppermute | solution.py:54
  34.8 0.0 collective-permute-done.5.refs_5_
  34.8 0.1 collective-permute-start.8
  34.9 0.0 collective-permute-done.3.refs_3_
  34.9 4.1 %collective-permute-start.9 = (bf16[4,192,128]{2,1,0:T(8,128)(2,1)S(1)}, bf16[4,192,128]{2,1,0:T(8,128)(2,1)S(1)}, u32[]{:S(2)}, u32[]{:S(2)}) collective-permute-start(bf16[4,192,128]{2,1,0:T(8,128)(2,1)S(1)} %collective-permute-done.3.refs_3_), channel_id=1, source_target_pairs={{2,4},{6,8},{10,12},{14,16},{18,20},{22,24},{26,28},{30,32},{34,36... | collective-permute-start | bytes 589832 | tf_op jit(solution)/shard_map/ppermute | solution.py:54
  39.0 0.0 collective-permute-done.7.refs_2_
  39.0 5.1 %collective-permute-start.11 = (bf16[4,128,128]{2,1,0:T(8,128)(2,1)S(1)}, bf16[4,128,128]{2,1,0:T(8,128)(2,1)S(1)}, u32[]{:S(2)}, u32[]{:S(2)}) collective-permute-start(bf16[4,128,128]{2,1,0:T(8,128)(2,1)S(1)} %copy-done.2), channel_id=1, source_target_pairs={{0,1},{1,0},{2,3},{3,2},{4,5},{5,4},{6,7},{7,6},{8,9},{9,8},{10,11... | collective-permute-start | bytes 393224 | tf_op jit(solution)/shard_map/ppermute | solution.py:50
  44.1 0.5 gather.2.refs_0_
  44.6 0.0 copy-done.3
  44.6 0.0 copy-start
  44.6 0.2 gather.3.window_in
  44.8 0.2 collective-permute-done.11.refs_7_
  45.1 0.0 collective-permute-done.8.refs_0_
  45.1 0.5 collective-permute-done.9.refs_1_
  45.5 0.0 collective-permute-done.10.refs_3_
  45.6 0.5 copy-done
  46.0 3.0 %reduce_and_solve.1 = (bf16[8,64,128]{2,1,0:T(8,128)(2,1)S(1)}, bf16[81,192,128]{2,1,0:T(8,128)(2,1)S(1)}) custom-call(s32[8,16]{1,0:T(8,128)S(1)} %get-tuple-element.22.table_ref, bf16[81,192,128]{2,1,0:T(8,128)(2,1)S(1)} %gather.3.window_in, bf16[4,192,128]{2,1,0:T(8,128)(2,1)S(1)} %collective-permute-done.8.refs_0_, ...), custom_call_target="tpu_custom_call", output_to_operand_aliasing={{1}: (1, {})} | custom-call | flops 402653184 | bytes 6000000 | tf_op jit(solution)/shard_map/reduce_and_solve/pallas_call | solution.py:277
  49.0 0.1 collective-permute-start.12
  49.1 8.3 %collective-permute-start.13 = (bf16[8,64,128]{2,1,0:T(8,128)(2,1)S(1)}, bf16[8,64,128]{2,1,0:T(8,128)(2,1)S(1)}, u32[]{:S(2)}, u32[]{:S(2)}) collective-permute-start(bf16[8,64,128]{2,1,0:T(8,128)(2,1)S(1)} %get-tuple-element.28.own_ref.refs_0_), channel_id=1, source_target_pairs={{2,4},{6,8},{10,12},{14,16},{18,20},{22,24},{26,28},{30,32},{34,36... | collective-permute-start | bytes 393224 | tf_op jit(solution)/shard_map/ppermute | solution.py:54
  57.5 0.1 collective-permute-start.14
  57.6 3.3 %collective-permute-start.15 = (bf16[8,64,128]{2,1,0:T(8,128)(2,1)S(1)}, bf16[8,64,128]{2,1,0:T(8,128)(2,1)S(1)}, u32[]{:S(2)}, u32[]{:S(2)}) collective-permute-start(bf16[8,64,128]{2,1,0:T(8,128)(2,1)S(1)} %get-tuple-element.28.own_ref.refs_0_), channel_id=1, source_target_pairs={{4,8},{6,10},{12,16},{14,18},{20,24},{22,26},{28,32},{30,34},{36,4... | collective-permute-start | bytes 393224 | tf_op jit(solution)/shard_map/ppermute | solution.py:54
  60.8 2.2 %fold.2 = (bf16[8,256,512]{2,1,0:T(8,128)(2,1)S(1)}, f32[8,64,256]{2,1,0:T(8,128)S(1)}, bf16[8,256,128]{2,1,0:T(8,128)(2,1)S(1)}) custom-call(bf16[4,192,128]{2,1,0:T(8,128)(2,1)S(1)} %get-tuple-element.23.refs_0_.elim_ref, bf16[8,192,192]{2,1,0:T(8,128)(2,1)S(1)} %get-tuple-element.29.inverse_ref, bf16[8,256,256]{2,1,0:T(8,128)(2,1)S(1)} %get-tuple-element.30.basis_ref, ...), custom_call_target="tpu_custom_call" | custom-call | flops 603979776 | bytes 8000000 | tf_op jit(solution)/shard_map/fold/pallas_call | solution.py:231
  63.1 0.0 collective-permute-done.16.backward_ref
  63.1 2.2 %fold.3 = (bf16[8,256,512]{2,1,0:T(8,128)(2,1)S(1)}, f32[8,64,256]{2,1,0:T(8,128)S(1)}, bf16[8,256,128]{2,1,0:T(8,128)(2,1)S(1)}) custom-call(bf16[4,192,128]{2,1,0:T(8,128)(2,1)S(1)} %get-tuple-element.25.refs_1_.elim_ref, bf16[8,192,192]{2,1,0:T(8,128)(2,1)S(1)} %collective-permute-done.1.inverse_ref, ...), custom_call_target="tpu_custom_call" | custom-call | flops 603979776 | bytes 8000000 | tf_op jit(solution)/shard_map/fold/pallas_call | solution.py:231
  65.3 0.5 add_own.1.refs_7_
  65.9 0.0 collective-permute-done.12.refs_1_
  65.9 0.0 collective-permute-done.13.refs_2_
  65.9 0.0 collective-permute-done.14.refs_3_
  65.9 5.9 %collective-permute-done.15.refs_4_ = bf16[8,64,128]{2,1,0:T(8,128)(2,1)S(1)} collective-permute-done((bf16[8,64,128]{2,1,0:T(8,128)(2,1)S(1)}, bf16[8,64,128]{2,1,0:T(8,128)(2,1)S(1)}, u32[]{:S(2)}, u32[]{:S(2)}) %collective-permute-start.15) | collective-permute-done | bytes 131104 | tf_op jit(solution)/shard_map/ppermute | solution.py:54
  71.8 3.1 %finish.1 = bf16[16,64,256]{2,1,0:T(8,128)(2,1)} custom-call(s32[8,16]{1,0:T(8,128)S(1)} %get-tuple-element.21.table_ref, bf16[8,64,128]{2,1,0:T(8,128)(2,1)S(1)} %get-tuple-element.28.own_ref.refs_0_, bf16[8,64,128]{2,1,0:T(8,128)(2,1)S(1)} %collective-permute-done.12.refs_1_, bf16[8,64,128]{2,1,0:T(8,128)(2,1)S(1)} %collective-permute-done.13.refs_2_, ...), custom_call_target="tpu_custom_call" | custom-call | flops 268435456 | bytes 6000000 | tf_op jit(solution)/shard_map/finish/pallas_call | solution.py:336
  (6 shorter events, 0.0 us)
Async XLA Ops:
  0.0 39.0 %copy-start.2 = (bf16[4,128,128]{2,1,0:T(8,128)(2,1)S(1)}, bf16[4,128,128]{2,1,0:T(8,128)(2,1)}, u32[]{:S(2)}) copy-start(bf16[4,128,128]{2,1,0:T(8,128)(2,1)} %refs_6_.1) | copy-start | bytes 393220
  0.0 45.5 %collective-permute-start.10 = (bf16[8,64,1536]{2,1,0:T(8,128)(2,1)}, bf16[8,64,1536]{2,1,0:T(8,128)(2,1)S(1)}, u32[]{:S(2)}, u32[]{:S(2)}) collective-permute-start(bf16[8,64,1536]{2,1,0:T(8,128)(2,1)} %refs_2_.1), channel_id=1, source_target_pairs={{0,1},{1,0},{2,3},{3,2},{4,5},{5,4},{6,7},{7,6},{8,9},{9,8},{10,11... | collective-permute-start | bytes 4718600 | tf_op jit(solution)/shard_map/ppermute | solution.py:50
  0.7 62.4 %collective-permute-start.16 = (bf16[8,192,512]{2,1,0:T(8,128)(2,1)}, bf16[8,192,512]{2,1,0:T(8,128)(2,1)S(1)}, u32[]{:S(2)}, u32[]{:S(2)}) collective-permute-start(bf16[8,192,512]{2,1,0:T(8,128)(2,1)} %backward_ref.1), channel_id=1, source_target_pairs={{0,1},{1,0},{2,3},{3,2},{4,5},{5,4},{6,7},{7,6},{8,9},{9,8},{10,11... | collective-permute-start | bytes 4718600 | tf_op jit(solution)/shard_map/ppermute | solution.py:50
  0.8 18.8 %collective-permute-start = (bf16[8,256,256]{2,1,0:T(8,128)(2,1)}, bf16[8,256,256]{2,1,0:T(8,128)(2,1)S(1)}, u32[]{:S(2)}, u32[]{:S(2)}) collective-permute-start(bf16[8,256,256]{2,1,0:T(8,128)(2,1)} %basis_hbm.1), channel_id=1, source_target_pairs={{0,1},{1,0},{2,3},{3,2},{4,5},{5,4},{6,7},{7,6},{8,9},{9,8},{10,11... | collective-permute-start | bytes 3145736 | tf_op jit(solution)/shard_map/ppermute | solution.py:50
  1.2 16.9 %collective-permute-start.1 = (bf16[8,192,192]{2,1,0:T(8,128)(2,1)}, bf16[8,192,192]{2,1,0:T(8,128)(2,1)S(1)}, u32[]{:S(2)}, u32[]{:S(2)}) collective-permute-start(bf16[8,192,192]{2,1,0:T(8,128)(2,1)} %inverse_hbm.1), channel_id=1, source_target_pairs={{0,1},{1,0},{2,3},{3,2},{4,5},{5,4},{6,7},{7,6},{8,9},{9,8},{10,11... | collective-permute-start | bytes 1769480 | tf_op jit(solution)/shard_map/ppermute | solution.py:50
  3.7 14.4 %collective-permute-start.4 = (bf16[4,192,128]{2,1,0:T(8,128)(2,1)S(1)}, bf16[4,192,128]{2,1,0:T(8,128)(2,1)S(1)}, u32[]{:S(2)}, u32[]{:S(2)}) collective-permute-start(bf16[4,192,128]{2,1,0:T(8,128)(2,1)S(1)} %get-tuple-element.23.refs_0_.elim_ref), channel_id=1, source_target_pairs={{2,4},{6,8},{10,12},{14,16},{18,20},{22,24},{26,28},{30,32},{34,36... | collective-permute-start | bytes 589832 | tf_op jit(solution)/shard_map/ppermute | solution.py:54
  18.1 9.6 %collective-permute-start.2 = (bf16[4,192,128]{2,1,0:T(8,128)(2,1)S(1)}, bf16[4,192,128]{2,1,0:T(8,128)(2,1)S(1)}, u32[]{:S(2)}, u32[]{:S(2)}) collective-permute-start(bf16[4,192,128]{2,1,0:T(8,128)(2,1)S(1)} %get-tuple-element.23.refs_0_.elim_ref), channel_id=1, source_target_pairs={{0,2},{4,6},{8,10},{12,14},{16,18},{20,22},{24,26},{28,30},{32,34}... | collective-permute-start | bytes 589832 | tf_op jit(solution)/shard_map/ppermute | solution.py:54
  18.1 9.7 %collective-permute-start.6 = (bf16[4,192,128]{2,1,0:T(8,128)(2,1)S(1)}, bf16[4,192,128]{2,1,0:T(8,128)(2,1)S(1)}, u32[]{:S(2)}, u32[]{:S(2)}) collective-permute-start(bf16[4,192,128]{2,1,0:T(8,128)(2,1)S(1)} %collective-permute-done.4.refs_4_), channel_id=1, source_target_pairs={{0,2},{4,6},{8,10},{12,14},{16,18},{20,22},{24,26},{28,30},{32,34}... | collective-permute-start | bytes 589832 | tf_op jit(solution)/shard_map/ppermute | solution.py:54
  20.3 24.2 %copy-start.3 = (s32[16,8]{0,1:T(8,128)S(1)}, s32[16,8]{0,1:T(8,128)}, u32[]{:S(2)}) copy-start(s32[16,8]{0,1:T(8,128)} %param.14) | copy-start | bytes 1540
  20.3 24.2 %copy-start.4 = (s32[16]{0:T(128)S(1)}, s32[16]{0:T(128)}, u32[]{:S(2)}) copy-start(s32[16]{0:T(128)} %param.15) | copy-start | bytes 196
  20.4 14.4 %collective-permute-start.5 = (bf16[4,192,128]{2,1,0:T(8,128)(2,1)S(1)}, bf16[4,192,128]{2,1,0:T(8,128)(2,1)S(1)}, u32[]{:S(2)}, u32[]{:S(2)}) collective-permute-start(bf16[4,192,128]{2,1,0:T(8,128)(2,1)S(1)} %get-tuple-element.25.refs_1_.elim_ref), channel_id=1, source_target_pairs={{2,4},{6,8},{10,12},{14,16},{18,20},{22,24},{26,28},{30,32},{34,36... | collective-permute-start | bytes 589832 | tf_op jit(solution)/shard_map/ppermute | solution.py:54
  27.7 7.2 %collective-permute-start.3 = (bf16[4,192,128]{2,1,0:T(8,128)(2,1)S(1)}, bf16[4,192,128]{2,1,0:T(8,128)(2,1)S(1)}, u32[]{:S(2)}, u32[]{:S(2)}) collective-permute-start(bf16[4,192,128]{2,1,0:T(8,128)(2,1)S(1)} %get-tuple-element.25.refs_1_.elim_ref), channel_id=1, source_target_pairs={{0,2},{4,6},{8,10},{12,14},{16,18},{20,22},{24,26},{28,30},{32,34}... | collective-permute-start | bytes 589832 | tf_op jit(solution)/shard_map/ppermute | solution.py:54
  27.8 11.2 %collective-permute-start.7 = (bf16[4,192,128]{2,1,0:T(8,128)(2,1)S(1)}, bf16[4,192,128]{2,1,0:T(8,128)(2,1)S(1)}, u32[]{:S(2)}, u32[]{:S(2)}) collective-permute-start(bf16[4,192,128]{2,1,0:T(8,128)(2,1)S(1)} %collective-permute-done.2.refs_2_), channel_id=1, source_target_pairs={{2,4},{6,8},{10,12},{14,16},{18,20},{22,24},{26,28},{30,32},{34,36... | collective-permute-start | bytes 589832 | tf_op jit(solution)/shard_map/ppermute | solution.py:54
  34.8 10.3 %collective-permute-start.8 = (bf16[4,192,128]{2,1,0:T(8,128)(2,1)S(1)}, bf16[4,192,128]{2,1,0:T(8,128)(2,1)S(1)}, u32[]{:S(2)}, u32[]{:S(2)}) collective-permute-start(bf16[4,192,128]{2,1,0:T(8,128)(2,1)S(1)} %collective-permute-done.5.refs_5_), channel_id=1, source_target_pairs={{0,2},{4,6},{8,10},{12,14},{16,18},{20,22},{24,26},{28,30},{32,34}... | collective-permute-start | bytes 589832 | tf_op jit(solution)/shard_map/ppermute | solution.py:54
  34.9 10.6 %collective-permute-start.9 = (bf16[4,192,128]{2,1,0:T(8,128)(2,1)S(1)}, bf16[4,192,128]{2,1,0:T(8,128)(2,1)S(1)}, u32[]{:S(2)}, u32[]{:S(2)}) collective-permute-start(bf16[4,192,128]{2,1,0:T(8,128)(2,1)S(1)} %collective-permute-done.3.refs_3_), channel_id=1, source_target_pairs={{2,4},{6,8},{10,12},{14,16},{18,20},{22,24},{26,28},{30,32},{34,36... | collective-permute-start | bytes 589832 | tf_op jit(solution)/shard_map/ppermute | solution.py:54
  39.0 6.1 %collective-permute-start.11 = (bf16[4,128,128]{2,1,0:T(8,128)(2,1)S(1)}, bf16[4,128,128]{2,1,0:T(8,128)(2,1)S(1)}, u32[]{:S(2)}, u32[]{:S(2)}) collective-permute-start(bf16[4,128,128]{2,1,0:T(8,128)(2,1)S(1)} %copy-done.2), channel_id=1, source_target_pairs={{0,1},{1,0},{2,3},{3,2},{4,5},{5,4},{6,7},{7,6},{8,9},{9,8},{10,11... | collective-permute-start | bytes 393224 | tf_op jit(solution)/shard_map/ppermute | solution.py:50
  44.6 1.4 %copy-start = (bf16[8,64,1536]{2,1,0:T(8,128)(2,1)S(1)}, bf16[8,64,1536]{2,1,0:T(8,128)(2,1)}, u32[]{:S(2)}) copy-start(bf16[8,64,1536]{2,1,0:T(8,128)(2,1)} %refs_2_.1) | copy-start | bytes 4718596
  46.0 14.8 %copy-start.1 = (bf16[8,192,512]{2,1,0:T(8,128)(2,1)S(1)}, bf16[8,192,512]{2,1,0:T(8,128)(2,1)}, u32[]{:S(2)}) copy-start(bf16[8,192,512]{2,1,0:T(8,128)(2,1)} %backward_ref.1) | copy-start | bytes 4718596
  49.0 16.8 %collective-permute-start.12 = (bf16[8,64,128]{2,1,0:T(8,128)(2,1)S(1)}, bf16[8,64,128]{2,1,0:T(8,128)(2,1)S(1)}, u32[]{:S(2)}, u32[]{:S(2)}) collective-permute-start(bf16[8,64,128]{2,1,0:T(8,128)(2,1)S(1)} %get-tuple-element.28.own_ref.refs_0_), channel_id=1, source_target_pairs={{0,2},{4,6},{8,10},{12,14},{16,18},{20,22},{24,26},{28,30},{32,34}... | collective-permute-start | bytes 393224 | tf_op jit(solution)/shard_map/ppermute | solution.py:54
  49.1 16.7 %collective-permute-start.13 = (bf16[8,64,128]{2,1,0:T(8,128)(2,1)S(1)}, bf16[8,64,128]{2,1,0:T(8,128)(2,1)S(1)}, u32[]{:S(2)}, u32[]{:S(2)}) collective-permute-start(bf16[8,64,128]{2,1,0:T(8,128)(2,1)S(1)} %get-tuple-element.28.own_ref.refs_0_), channel_id=1, source_target_pairs={{2,4},{6,8},{10,12},{14,16},{18,20},{22,24},{26,28},{30,32},{34,36... | collective-permute-start | bytes 393224 | tf_op jit(solution)/shard_map/ppermute | solution.py:54
  57.5 8.4 %collective-permute-start.14 = (bf16[8,64,128]{2,1,0:T(8,128)(2,1)S(1)}, bf16[8,64,128]{2,1,0:T(8,128)(2,1)S(1)}, u32[]{:S(2)}, u32[]{:S(2)}) collective-permute-start(bf16[8,64,128]{2,1,0:T(8,128)(2,1)S(1)} %get-tuple-element.28.own_ref.refs_0_), channel_id=1, source_target_pairs={{0,4},{2,6},{8,12},{10,14},{16,20},{18,22},{24,28},{26,30},{32,36}... | collective-permute-start | bytes 393224 | tf_op jit(solution)/shard_map/ppermute | solution.py:54
  57.6 14.3 %collective-permute-start.15 = (bf16[8,64,128]{2,1,0:T(8,128)(2,1)S(1)}, bf16[8,64,128]{2,1,0:T(8,128)(2,1)S(1)}, u32[]{:S(2)}, u32[]{:S(2)}) collective-permute-start(bf16[8,64,128]{2,1,0:T(8,128)(2,1)S(1)} %get-tuple-element.28.own_ref.refs_0_), channel_id=1, source_target_pairs={{4,8},{6,10},{12,16},{14,18},{20,24},{22,26},{28,32},{30,34},{36,4... | collective-permute-start | bytes 393224 | tf_op jit(solution)/shard_map/ppermute | solution.py:54

commit v2 on v1

--- a/solution.py
+++ b/solution.py
@@ -13,6 +13,7 @@
 F32 = jnp.float32
 BF16 = jnp.bfloat16
 NT = (((1,), (1,)), ((), ()))
+TN = (((0,), (0,)), ((), ()))
 SMEM = pl.BlockSpec(memory_space=pltpu.SMEM)
 VMEM = pl.BlockSpec(memory_space=pltpu.VMEM)
 HBM = pl.BlockSpec(memory_space=pltpu.HBM)
@@ -201,7 +202,7 @@
     operands = blocks if fresh else (window,) + blocks
     return pl.pallas_call(
         functools.partial(gather_kernel, firsts, fresh),
-        out_shape=shape(2 * ROWS + 1, 192, 128),
+        out_shape=shape(2 * ROWS + 1, *blocks[0].shape[1:]),
         in_specs=[VMEM] * len(operands),
         out_specs=VMEM,
         input_output_aliases={} if fresh else {0: 0},
@@ -218,11 +219,13 @@
         for t in range(2):
             j = 2 * pair + t
             both = lax.dot_general(
-                basis_ref[j][:, :redundant], inverse_ref[j], NT, preferred_element_type=F32
+                inverse_ref[j], basis_ref[j][:, :redundant], NT, preferred_element_type=F32
             ).astype(BF16)
-            wide_ref[j] = jnp.dot(both, backward_ref[j], preferred_element_type=F32).astype(BF16)
-            base_ref[j] = lax.dot_general(
-                elim[t * HALF : (t + 1) * HALF, :], both, NT, preferred_element_type=F32
+            wide_ref[j] = lax.dot_general(
+                backward_ref[j], both, TN, preferred_element_type=F32
+            ).astype(BF16)
+            base_ref[j] = jnp.dot(
+                elim[t * HALF : (t + 1) * HALF, :], both, preferred_element_type=F32
             )
             tail_ref[j] = basis_ref[j][:, 128:]
 
@@ -230,7 +233,7 @@
 def fold(elim, inverse, basis, backward):
     return pl.pallas_call(
         fold_kernel,
-        out_shape=(shape(8, 256, 512), shape(8, 64, 256, dtype=F32), shape(8, 256, 128)),
+        out_shape=(shape(8, 512, 256), shape(8, 64, 256, dtype=F32), shape(8, 256, 128)),
         in_specs=[VMEM] * 4,
         out_specs=[VMEM] * 3,
         name="fold",
@@ -240,14 +243,11 @@
 
 
 def reduce_kernel(table_ref, window_in, *refs):
-    blocks = refs[:2]
-    f_refs = refs[2:4]
-    skel_refs = refs[4:6]
-    parent_refs = refs[6:8]
-    out_ref, window = refs[8:]
+    last_ref, *refs = refs
+    f_refs, skel_refs, parent_refs = refs[:2], refs[2:4], refs[4:6]
+    out_ref, window = refs[6:]
     core = lax.axis_index("rhs")
-    for first, block in zip((28, 36), blocks):
-        place_block(window, block, first)
+    place_block(window, last_ref, 36)
     low = low_lanes()
     for h in range(2):
         for two in range(2):
@@ -273,17 +273,17 @@
                 out_ref[4 * h + 2 * two + parity] = both[parity * HALF : (parity + 1) * HALF, :]
 
 
-def reduce_and_solve(table, window, blocks, forward, skel, parent):
+def reduce_and_solve(table, window, last, forward, skel, parent):
     return pl.pallas_call(
         reduce_kernel,
         out_shape=(shape(8, 64, 128), shape(*window.shape)),
-        in_specs=[SMEM] + [VMEM] * 9,
+        in_specs=[SMEM] + [VMEM] * 8,
         out_specs=[VMEM] * 2,
         input_output_aliases={1: 1},
         name="reduce_and_solve",
         cost_estimate=cost(2 * 16 * 64 * 1536 * 128, 6000000),
         compiler_params=limit(6),
-    )(table, window, *blocks, *forward, *skel, *parent)[0]
+    )(table, window, last, *forward, *skel, *parent)[0]
 
 
 def own_kernel(own_ref, *refs):
@@ -312,13 +312,13 @@
     )(own, *tails, *base)
 
 
-def finish_kernel(table_ref, *refs):
-    blocks, wide_refs, base_ref, out_ref, window = refs[:5], refs[5:7], refs[7], refs[8], refs[9]
-    for n, block in enumerate(blocks):
-        place_block(window, block, 8 * n)
-    window[2 * ROWS] = jnp.zeros(window.shape[1:], BF16)
+def finish_kernel(row, table_ref, window_in, last_ref, *refs):
+    wide_refs, base_ref = refs[:2], refs[2]
+    out_hbm, window, out_ref, sems = refs[3:]
+    place_block(window, last_ref, row)
     core = lax.axis_index("rhs")
     low = low_lanes()
+    copies = []
     for h in range(2):
         for j in range(8):
             cluster = (core ^ h) * 8 + j
@@ -326,23 +326,29 @@
             for k in range(0, 8, 2):
                 left, right = window[table_ref[k, cluster]], window[table_ref[k + 1, cluster]]
                 parts.append(jnp.where(low, left, right))
-            carried = lax.dot_general(
-                jnp.concatenate(parts, axis=1), wide_refs[h][j], NT, preferred_element_type=F32
+            carried = jnp.dot(
+                jnp.concatenate(parts, axis=1), wide_refs[h][j], preferred_element_type=F32
             )
-            out_ref[cluster] = (base_ref[8 * h + j] - carried).astype(BF16)
-
-
-def finish(table, blocks, wide, base):
-    return pl.pallas_call(
-        finish_kernel,
-        out_shape=shape(16, 64, 256),
-        in_specs=[SMEM] + [VMEM] * 8,
-        out_specs=VMEM,
-        scratch_shapes=[pltpu.VMEM((2 * ROWS + 1, 64, 128), BF16)],
+            out_ref[8 * h + j] = (base_ref[8 * h + j] - carried).astype(BF16)
+        here = pl.ds((core ^ h) * 8, 8)
+        copies.append(pltpu.make_async_copy(out_ref.at[pl.ds(8 * h, 8)], out_hbm.at[here], sems.at[h]))
+        copies[h].start()
+    for copy in copies:
+        copy.wait()
+
+
+def finish(row, table, window, last, wide, base):
+    return pl.pallas_call(
+        functools.partial(finish_kernel, row),
+        out_shape=(shape(*base.shape), shape(*window.shape)),
+        in_specs=[SMEM] + [VMEM] * 5,
+        out_specs=(HBM, VMEM),
+        scratch_shapes=[pltpu.VMEM(base.shape, BF16), pltpu.SemaphoreType.DMA((2,))],
+        input_output_aliases={1: 1},
         name="finish",
         cost_estimate=cost(2 * 16 * 64 * 512 * 256, 6000000),
-        compiler_params=limit(6),
-    )(table, *blocks, *wide, base)
+        compiler_params=pltpu.CompilerParams(vmem_limit_bytes=6 << 20),
+    )(table, window, last, *wide, base)[0]
 
 
 def on_device(
@@ -375,16 +381,18 @@
     window_blocks = (elim_a, elim_b, inner_a, inner_b, outer_a, outer_b)
     window = gather((0, 4, 8, 12, 16, 20), window_blocks)
     window = gather((24, 32), (far_inner_a, far_outer_a), window)
+    window = gather((28,), (far_inner_b,), window)
     wide_a, base_a, tail_a = fold(elim_a, inverse_a, basis_a, backward_coupling)
     wide_b, base_b, tail_b = fold(elim_b, inverse_b, basis_b, backward_b)
     factors = (forward_coupling, forward_b), (skel_a, skel_b), (parent_inverse, parent_b)
-    skeleton = reduce_and_solve(forward_table, window, (far_inner_b, far_outer_b), *factors)
+    skeleton = reduce_and_solve(forward_table, window, far_outer_b, *factors)
     near_s = along(skeleton, near)
     inner_s = along(skeleton, inner)
     far_s = along(skeleton, far)
     outer_s = along(skeleton, outer)
     base = add_own(skeleton, (tail_a, tail_b), (base_a, base_b))
-    return finish(backward_table, (skeleton, inner_s, outer_s, near_s, far_s), (wide_a, wide_b), base)
+    window = gather((0, 8, 16, 32), (skeleton, inner_s, outer_s, far_s))
+    return finish(24, backward_table, window, near_s, (wide_a, wide_b), base)
 
 
 def solution(mesh):

time: 75.5 us -> 73.7 us (0.976)
  waiting for transfers between devices: 11.5 us -> 8.63 us
    ppermute x12, waiting for transfers between devices: 11.3 us -> 8.52 us  [along(): return lax.ppermute(value, 'leaf', pairs)]
  transfers between devices with their start and end apart: 17 -> 17, of which waited for: 4 -> 4; matrix products, arithmetic and copies ran while one was open for 0% -> 0% of each run, Pallas kernels for 16% -> 18%
where the time goes in v2:
time: 73.7 us; the launch traced here: 72.7 us
  starting transfers between devices  47.7 us (65%)
  Pallas kernels  15.2 us (21%)
  waiting for transfers between devices  8.63 us (12%)
    ppermute x12, starting transfers between devices, along(): return lax.ppermute(value, 'leaf', pairs)  41.4 us
    ppermute x12, waiting for transfers between devices, along(): return lax.ppermute(value, 'leaf', pairs)  8.52 us
    ppermute x5, starting transfers between devices, swap(): return lax.ppermute(value, 'rhs', [(0, 1), (1, 0)])  6.35 us
    pallas_call x2, Pallas kernels, fold(): pl.pallas_call(fold_kernel, out_shape=(shape(8, 512, 256), shape(8, 64, 2...  5.3 us
    pallas_call x1, Pallas kernels, reduce_and_solve(): pl.pallas_call(reduce_kernel, out_shape=(shape(8, 64, 128), shape(*window...  2.92 us
    pallas_call x1, Pallas kernels, project_own(): pl.pallas_call(project_own_kernel, out_shape=[shape(4, 192, 128), shape(4...  2.41 us
    pallas_call x1, Pallas kernels, finish(): pl.pallas_call(functools.partial(finish_kernel, row), out_shape=(shape(*b...  2.24 us
  transfers between devices with their start and end apart: 17, of which 4 were waited for; matrix products, arithmetic and copies ran while one was open for 0% of the time, Pallas kernels for 18%

profile of v2, /device:TPU:9, one launch (start us, length us, event | category | flops | bytes accessed | tf_op | source)
XLA Modules:
  0.0 72.7 jit_solution(9017340699822802035)
XLA Ops:
  0.0 0.7 collective-permute-start.10
  0.7 0.1 collective-permute-start.16
  0.8 0.4 collective-permute-start
  1.2 0.1 collective-permute-start.1
  1.3 2.4 %project_own.1 = (bf16[4,192,128]{2,1,0:T(8,128)(2,1)S(1)}, f32[4,64,128]{2,1,0:T(8,128)S(1)}, bf16[8,64,256]{2,1,0:T(8,128)(2,1)S(1)}, bf16[8,256,256]{2,1,0:T(8,128)(2,1)S(1)}, bf16[8,192,192]{2,1,0:T(8,128)(2,1)S(1)}) custom-call(bf16[16,64,256]{2,1,0:T(8,128)(2,1)} %rhs_hbm.1, bf16[8,256,256]{2,1,0:T(8,128)(2,1)} %basis_hbm.1, ...), custom_call_target="tpu_custom_call" | custom-call | flops 104857600 | bytes 2500000 | tf_op jit(solution)/shard_map/project_own/pallas_call | solution.py:145
  3.7 9.6 %collective-permute-start.4 = (bf16[4,192,128]{2,1,0:T(8,128)(2,1)S(1)}, bf16[4,192,128]{2,1,0:T(8,128)(2,1)S(1)}, u32[]{:S(2)}, u32[]{:S(2)}) collective-permute-start(bf16[4,192,128]{2,1,0:T(8,128)(2,1)S(1)} %get-tuple-element.24.refs_0_.elim_ref), channel_id=1, source_target_pairs={{2,4},{6,8},{10,12},{14,16},{18,20},{22,24},{26,28},{30,32},{34,36... | collective-permute-start | bytes 589832 | tf_op jit(solution)/shard_map/ppermute | solution.py:55
  13.3 4.8 %collective-permute-done.4.refs_4_ = bf16[4,192,128]{2,1,0:T(8,128)(2,1)S(1)} collective-permute-done((bf16[4,192,128]{2,1,0:T(8,128)(2,1)S(1)}, bf16[4,192,128]{2,1,0:T(8,128)(2,1)S(1)}, u32[]{:S(2)}, u32[]{:S(2)}) %collective-permute-start.4) | collective-permute-done | bytes 196640 | tf_op jit(solution)/shard_map/ppermute | solution.py:55
  18.1 0.0 collective-permute-start.2
  18.1 0.0 collective-permute-done.1.inverse_ref
  18.1 1.5 %collective-permute-start.6 = (bf16[4,192,128]{2,1,0:T(8,128)(2,1)S(1)}, bf16[4,192,128]{2,1,0:T(8,128)(2,1)S(1)}, u32[]{:S(2)}, u32[]{:S(2)}) collective-permute-start(bf16[4,192,128]{2,1,0:T(8,128)(2,1)S(1)} %collective-permute-done.4.refs_4_), channel_id=1, source_target_pairs={{0,2},{4,6},{8,10},{12,14},{16,18},{20,22},{24,26},{28,30},{32,34}... | collective-permute-start | bytes 589832 | tf_op jit(solution)/shard_map/ppermute | solution.py:55
  19.6 0.0 collective-permute-done.basis_ref
  19.6 0.7 %project_other.1 = (bf16[4,192,128]{2,1,0:T(8,128)(2,1)S(1)}, f32[4,64,128]{2,1,0:T(8,128)S(1)}) custom-call(bf16[8,64,256]{2,1,0:T(8,128)(2,1)S(1)} %get-tuple-element.25.rhs_ref, bf16[8,256,256]{2,1,0:T(8,128)(2,1)S(1)} %collective-permute-done.basis_ref, bf16[8,192,192]{2,1,0:T(8,128)(2,1)S(1)} %collective-permute-done.1.inverse_ref), custom_call_target="tpu_custom_call" | custom-call | flops 104857600 | bytes 2500000 | tf_op jit(solution)/shard_map/project_other/pallas_call | solution.py:173
  20.3 0.0 copy-start.3
  20.3 0.0 copy-start.4
  20.3 7.3 %collective-permute-start.5 = (bf16[4,192,128]{2,1,0:T(8,128)(2,1)S(1)}, bf16[4,192,128]{2,1,0:T(8,128)(2,1)S(1)}, u32[]{:S(2)}, u32[]{:S(2)}) collective-permute-start(bf16[4,192,128]{2,1,0:T(8,128)(2,1)S(1)} %get-tuple-element.26.refs_1_.elim_ref), channel_id=1, source_target_pairs={{2,4},{6,8},{10,12},{14,16},{18,20},{22,24},{26,28},{30,32},{34,36... | collective-permute-start | bytes 589832 | tf_op jit(solution)/shard_map/ppermute | solution.py:55
  27.6 0.0 collective-permute-done.2.refs_2_
  27.6 0.1 collective-permute-start.3
  27.7 0.0 collective-permute-done.6.refs_1_
  27.8 7.0 %collective-permute-start.7 = (bf16[4,192,128]{2,1,0:T(8,128)(2,1)S(1)}, bf16[4,192,128]{2,1,0:T(8,128)(2,1)S(1)}, u32[]{:S(2)}, u32[]{:S(2)}) collective-permute-start(bf16[4,192,128]{2,1,0:T(8,128)(2,1)S(1)} %collective-permute-done.2.refs_2_), channel_id=1, source_target_pairs={{2,4},{6,8},{10,12},{14,16},{18,20},{22,24},{26,28},{30,32},{34,36... | collective-permute-start | bytes 589832 | tf_op jit(solution)/shard_map/ppermute | solution.py:55
  34.8 0.0 collective-permute-done.5.refs_5_
  34.8 0.1 collective-permute-start.8
  34.9 0.0 collective-permute-done.3.refs_3_
  34.9 4.1 %collective-permute-start.9 = (bf16[4,192,128]{2,1,0:T(8,128)(2,1)S(1)}, bf16[4,192,128]{2,1,0:T(8,128)(2,1)S(1)}, u32[]{:S(2)}, u32[]{:S(2)}) collective-permute-start(bf16[4,192,128]{2,1,0:T(8,128)(2,1)S(1)} %collective-permute-done.3.refs_3_), channel_id=1, source_target_pairs={{2,4},{6,8},{10,12},{14,16},{18,20},{22,24},{26,28},{30,32},{34,36... | collective-permute-start | bytes 589832 | tf_op jit(solution)/shard_map/ppermute | solution.py:55
  39.0 0.0 collective-permute-done.7.refs_2_
  39.0 5.1 %collective-permute-start.11 = (bf16[4,128,128]{2,1,0:T(8,128)(2,1)S(1)}, bf16[4,128,128]{2,1,0:T(8,128)(2,1)S(1)}, u32[]{:S(2)}, u32[]{:S(2)}) collective-permute-start(bf16[4,128,128]{2,1,0:T(8,128)(2,1)S(1)} %copy-done.2), channel_id=1, source_target_pairs={{0,1},{1,0},{2,3},{3,2},{4,5},{5,4},{6,7},{7,6},{8,9},{9,8},{10,11... | collective-permute-start | bytes 393224 | tf_op jit(solution)/shard_map/ppermute | solution.py:51
  44.1 0.5 gather.4.refs_0_
  44.6 0.2 gather.5.refs_0_
  44.8 0.0 copy-start
  44.8 0.0 collective-permute-done.8.refs_1_
  44.8 0.1 gather.6.window_in
  45.0 0.1 collective-permute-done.11.refs_6_
  45.1 0.5 collective-permute-done.9.refs_0_
  45.5 0.0 collective-permute-done.10.refs_2_
  45.5 0.7 copy-done
  46.2 2.9 %reduce_and_solve.1 = (bf16[8,64,128]{2,1,0:T(8,128)(2,1)S(1)}, bf16[81,192,128]{2,1,0:T(8,128)(2,1)S(1)}) custom-call(s32[8,16]{1,0:T(8,128)S(1)} %get-tuple-element.23.table_ref, bf16[81,192,128]{2,1,0:T(8,128)(2,1)S(1)} %gather.6.window_in, bf16[4,192,128]{2,1,0:T(8,128)(2,1)S(1)} %collective-permute-done.9.refs_0_, ...), custom_call_target="tpu_custom_call", output_to_operand_aliasing={{1}: (1, {})} | custom-call | flops 402653184 | bytes 6000000 | tf_op jit(solution)/shard_map/reduce_and_solve/pallas_call | solution.py:277
  49.2 0.1 collective-permute-start.12
  49.3 8.3 %collective-permute-start.13 = (bf16[8,64,128]{2,1,0:T(8,128)(2,1)S(1)}, bf16[8,64,128]{2,1,0:T(8,128)(2,1)S(1)}, u32[]{:S(2)}, u32[]{:S(2)}) collective-permute-start(bf16[8,64,128]{2,1,0:T(8,128)(2,1)S(1)} %get-tuple-element.29.refs_0_.own_ref), channel_id=1, source_target_pairs={{2,4},{6,8},{10,12},{14,16},{18,20},{22,24},{26,28},{30,32},{34,36... | collective-permute-start | bytes 393224 | tf_op jit(solution)/shard_map/ppermute | solution.py:55
  57.6 3.1 %collective-permute-start.14 = (bf16[8,64,128]{2,1,0:T(8,128)(2,1)S(1)}, bf16[8,64,128]{2,1,0:T(8,128)(2,1)S(1)}, u32[]{:S(2)}, u32[]{:S(2)}) collective-permute-start(bf16[8,64,128]{2,1,0:T(8,128)(2,1)S(1)} %get-tuple-element.29.refs_0_.own_ref), channel_id=1, source_target_pairs={{4,8},{6,10},{12,16},{14,18},{20,24},{22,26},{28,32},{30,34},{36,4... | collective-permute-start | bytes 393224 | tf_op jit(solution)/shard_map/ppermute | solution.py:55
  60.7 0.3 collective-permute-start.15
  61.0 2.7 %fold.2 = (bf16[8,512,256]{2,1,0:T(8,128)(2,1)S(1)}, f32[8,64,256]{2,1,0:T(8,128)S(1)}, bf16[8,256,128]{2,1,0:T(8,128)(2,1)S(1)}) custom-call(bf16[4,192,128]{2,1,0:T(8,128)(2,1)S(1)} %get-tuple-element.24.refs_0_.elim_ref, bf16[8,192,192]{2,1,0:T(8,128)(2,1)S(1)} %get-tuple-element.30.inverse_ref, bf16[8,256,256]{2,1,0:T(8,128)(2,1)S(1)} %get-tuple-element.31.basis_ref, ...), custom_call_target="tpu_custom_call" | custom-call | flops 603979776 | bytes 8000000 | tf_op jit(solution)/shard_map/fold/pallas_call | solution.py:234
  63.6 2.6 %fold.3 = (bf16[8,512,256]{2,1,0:T(8,128)(2,1)S(1)}, f32[8,64,256]{2,1,0:T(8,128)S(1)}, bf16[8,256,128]{2,1,0:T(8,128)(2,1)S(1)}) custom-call(bf16[4,192,128]{2,1,0:T(8,128)(2,1)S(1)} %get-tuple-element.26.refs_1_.elim_ref, bf16[8,192,192]{2,1,0:T(8,128)(2,1)S(1)} %collective-permute-done.1.inverse_ref, ...), custom_call_target="tpu_custom_call" | custom-call | flops 603979776 | bytes 8000000 | tf_op jit(solution)/shard_map/fold/pallas_call | solution.py:234
  66.3 0.5 add_own.1.refs_2_
  66.8 0.0 collective-permute-done.12.refs_1_
  66.8 0.0 collective-permute-done.13.refs_2_
  66.8 3.2 %collective-permute-done.14.refs_3_ = bf16[8,64,128]{2,1,0:T(8,128)(2,1)S(1)} collective-permute-done((bf16[8,64,128]{2,1,0:T(8,128)(2,1)S(1)}, bf16[8,64,128]{2,1,0:T(8,128)(2,1)S(1)}, u32[]{:S(2)}, u32[]{:S(2)}) %collective-permute-start.14) | collective-permute-done | bytes 131104 | tf_op jit(solution)/shard_map/ppermute | solution.py:55
  70.0 0.2 gather.7.window_in
  70.3 0.0 collective-permute-done.15.last_ref
  70.3 2.2 %finish.1 = (bf16[16,64,256]{2,1,0:T(8,128)(2,1)}, bf16[81,64,128]{2,1,0:T(8,128)(2,1)S(1)}) custom-call(s32[8,16]{1,0:T(8,128)S(1)} %get-tuple-element.22.table_ref, bf16[81,64,128]{2,1,0:T(8,128)(2,1)S(1)} %gather.7.window_in, bf16[8,64,128]{2,1,0:T(8,128)(2,1)S(1)} %collective-permute-done.15.last_ref, ...), custom_call_target="tpu_custom_call", output_to_operand_aliasing={{1}: (1, {})} | custom-call | flops 268435456 | bytes 6000000 | tf_op jit(solution)/shard_map/finish/pallas_call | solution.py:341
  (8 shorter events, 0.0 us)
Async XLA Ops:
  0.0 39.0 %copy-start.2 = (bf16[4,128,128]{2,1,0:T(8,128)(2,1)S(1)}, bf16[4,128,128]{2,1,0:T(8,128)(2,1)}, u32[]{:S(2)}) copy-start(bf16[4,128,128]{2,1,0:T(8,128)(2,1)} %refs_5_.1) | copy-start | bytes 393220
  0.0 45.5 %collective-permute-start.10 = (bf16[8,64,1536]{2,1,0:T(8,128)(2,1)}, bf16[8,64,1536]{2,1,0:T(8,128)(2,1)S(1)}, u32[]{:S(2)}, u32[]{:S(2)}) collective-permute-start(bf16[8,64,1536]{2,1,0:T(8,128)(2,1)} %refs_1_.1), channel_id=1, source_target_pairs={{0,1},{1,0},{2,3},{3,2},{4,5},{5,4},{6,7},{7,6},{8,9},{9,8},{10,11... | collective-permute-start | bytes 4718600 | tf_op jit(solution)/shard_map/ppermute | solution.py:51
  0.7 63.0 %collective-permute-start.16 = (bf16[8,192,512]{2,1,0:T(8,128)(2,1)}, bf16[8,192,512]{2,1,0:T(8,128)(2,1)S(1)}, u32[]{:S(2)}, u32[]{:S(2)}) collective-permute-start(bf16[8,192,512]{2,1,0:T(8,128)(2,1)} %backward_ref.1), channel_id=1, source_target_pairs={{0,1},{1,0},{2,3},{3,2},{4,5},{5,4},{6,7},{7,6},{8,9},{9,8},{10,11... | collective-permute-start | bytes 4718600 | tf_op jit(solution)/shard_map/ppermute | solution.py:51
  0.8 18.8 %collective-permute-start = (bf16[8,256,256]{2,1,0:T(8,128)(2,1)}, bf16[8,256,256]{2,1,0:T(8,128)(2,1)S(1)}, u32[]{:S(2)}, u32[]{:S(2)}) collective-permute-start(bf16[8,256,256]{2,1,0:T(8,128)(2,1)} %basis_hbm.1), channel_id=1, source_target_pairs={{0,1},{1,0},{2,3},{3,2},{4,5},{5,4},{6,7},{7,6},{8,9},{9,8},{10,11... | collective-permute-start | bytes 3145736 | tf_op jit(solution)/shard_map/ppermute | solution.py:51
  1.2 16.9 %collective-permute-start.1 = (bf16[8,192,192]{2,1,0:T(8,128)(2,1)}, bf16[8,192,192]{2,1,0:T(8,128)(2,1)S(1)}, u32[]{:S(2)}, u32[]{:S(2)}) collective-permute-start(bf16[8,192,192]{2,1,0:T(8,128)(2,1)} %inverse_hbm.1), channel_id=1, source_target_pairs={{0,1},{1,0},{2,3},{3,2},{4,5},{5,4},{6,7},{7,6},{8,9},{9,8},{10,11... | collective-permute-start | bytes 1769480 | tf_op jit(solution)/shard_map/ppermute | solution.py:51
  3.7 14.4 %collective-permute-start.4 = (bf16[4,192,128]{2,1,0:T(8,128)(2,1)S(1)}, bf16[4,192,128]{2,1,0:T(8,128)(2,1)S(1)}, u32[]{:S(2)}, u32[]{:S(2)}) collective-permute-start(bf16[4,192,128]{2,1,0:T(8,128)(2,1)S(1)} %get-tuple-element.24.refs_0_.elim_ref), channel_id=1, source_target_pairs={{2,4},{6,8},{10,12},{14,16},{18,20},{22,24},{26,28},{30,32},{34,36... | collective-permute-start | bytes 589832 | tf_op jit(solution)/shard_map/ppermute | solution.py:55
  18.1 9.5 %collective-permute-start.2 = (bf16[4,192,128]{2,1,0:T(8,128)(2,1)S(1)}, bf16[4,192,128]{2,1,0:T(8,128)(2,1)S(1)}, u32[]{:S(2)}, u32[]{:S(2)}) collective-permute-start(bf16[4,192,128]{2,1,0:T(8,128)(2,1)S(1)} %get-tuple-element.24.refs_0_.elim_ref), channel_id=1, source_target_pairs={{0,2},{4,6},{8,10},{12,14},{16,18},{20,22},{24,26},{28,30},{32,34}... | collective-permute-start | bytes 589832 | tf_op jit(solution)/shard_map/ppermute | solution.py:55
  18.1 9.7 %collective-permute-start.6 = (bf16[4,192,128]{2,1,0:T(8,128)(2,1)S(1)}, bf16[4,192,128]{2,1,0:T(8,128)(2,1)S(1)}, u32[]{:S(2)}, u32[]{:S(2)}) collective-permute-start(bf16[4,192,128]{2,1,0:T(8,128)(2,1)S(1)} %collective-permute-done.4.refs_4_), channel_id=1, source_target_pairs={{0,2},{4,6},{8,10},{12,14},{16,18},{20,22},{24,26},{28,30},{32,34}... | collective-permute-start | bytes 589832 | tf_op jit(solution)/shard_map/ppermute | solution.py:55
  20.3 24.3 %copy-start.3 = (s32[16,8]{0,1:T(8,128)S(1)}, s32[16,8]{0,1:T(8,128)}, u32[]{:S(2)}) copy-start(s32[16,8]{0,1:T(8,128)} %param.14) | copy-start | bytes 1540
  20.3 24.3 %copy-start.4 = (s32[16]{0:T(128)S(1)}, s32[16]{0:T(128)}, u32[]{:S(2)}) copy-start(s32[16]{0:T(128)} %param.15) | copy-start | bytes 196
  20.3 14.5 %collective-permute-start.5 = (bf16[4,192,128]{2,1,0:T(8,128)(2,1)S(1)}, bf16[4,192,128]{2,1,0:T(8,128)(2,1)S(1)}, u32[]{:S(2)}, u32[]{:S(2)}) collective-permute-start(bf16[4,192,128]{2,1,0:T(8,128)(2,1)S(1)} %get-tuple-element.26.refs_1_.elim_ref), channel_id=1, source_target_pairs={{2,4},{6,8},{10,12},{14,16},{18,20},{22,24},{26,28},{30,32},{34,36... | collective-permute-start | bytes 589832 | tf_op jit(solution)/shard_map/ppermute | solution.py:55
  27.6 7.2 %collective-permute-start.3 = (bf16[4,192,128]{2,1,0:T(8,128)(2,1)S(1)}, bf16[4,192,128]{2,1,0:T(8,128)(2,1)S(1)}, u32[]{:S(2)}, u32[]{:S(2)}) collective-permute-start(bf16[4,192,128]{2,1,0:T(8,128)(2,1)S(1)} %get-tuple-element.26.refs_1_.elim_ref), channel_id=1, source_target_pairs={{0,2},{4,6},{8,10},{12,14},{16,18},{20,22},{24,26},{28,30},{32,34}... | collective-permute-start | bytes 589832 | tf_op jit(solution)/shard_map/ppermute | solution.py:55
  27.8 11.2 %collective-permute-start.7 = (bf16[4,192,128]{2,1,0:T(8,128)(2,1)S(1)}, bf16[4,192,128]{2,1,0:T(8,128)(2,1)S(1)}, u32[]{:S(2)}, u32[]{:S(2)}) collective-permute-start(bf16[4,192,128]{2,1,0:T(8,128)(2,1)S(1)} %collective-permute-done.2.refs_2_), channel_id=1, source_target_pairs={{2,4},{6,8},{10,12},{14,16},{18,20},{22,24},{26,28},{30,32},{34,36... | collective-permute-start | bytes 589832 | tf_op jit(solution)/shard_map/ppermute | solution.py:55
  34.8 10.0 %collective-permute-start.8 = (bf16[4,192,128]{2,1,0:T(8,128)(2,1)S(1)}, bf16[4,192,128]{2,1,0:T(8,128)(2,1)S(1)}, u32[]{:S(2)}, u32[]{:S(2)}) collective-permute-start(bf16[4,192,128]{2,1,0:T(8,128)(2,1)S(1)} %collective-permute-done.5.refs_5_), channel_id=1, source_target_pairs={{0,2},{4,6},{8,10},{12,14},{16,18},{20,22},{24,26},{28,30},{32,34}... | collective-permute-start | bytes 589832 | tf_op jit(solution)/shard_map/ppermute | solution.py:55
  34.9 10.6 %collective-permute-start.9 = (bf16[4,192,128]{2,1,0:T(8,128)(2,1)S(1)}, bf16[4,192,128]{2,1,0:T(8,128)(2,1)S(1)}, u32[]{:S(2)}, u32[]{:S(2)}) collective-permute-start(bf16[4,192,128]{2,1,0:T(8,128)(2,1)S(1)} %collective-permute-done.3.refs_3_), channel_id=1, source_target_pairs={{2,4},{6,8},{10,12},{14,16},{18,20},{22,24},{26,28},{30,32},{34,36... | collective-permute-start | bytes 589832 | tf_op jit(solution)/shard_map/ppermute | solution.py:55
  39.0 6.1 %collective-permute-start.11 = (bf16[4,128,128]{2,1,0:T(8,128)(2,1)S(1)}, bf16[4,128,128]{2,1,0:T(8,128)(2,1)S(1)}, u32[]{:S(2)}, u32[]{:S(2)}) collective-permute-start(bf16[4,128,128]{2,1,0:T(8,128)(2,1)S(1)} %copy-done.2), channel_id=1, source_target_pairs={{0,1},{1,0},{2,3},{3,2},{4,5},{5,4},{6,7},{7,6},{8,9},{9,8},{10,11... | collective-permute-start | bytes 393224 | tf_op jit(solution)/shard_map/ppermute | solution.py:51
  44.8 1.4 %copy-start = (bf16[8,64,1536]{2,1,0:T(8,128)(2,1)S(1)}, bf16[8,64,1536]{2,1,0:T(8,128)(2,1)}, u32[]{:S(2)}) copy-start(bf16[8,64,1536]{2,1,0:T(8,128)(2,1)} %refs_1_.1) | copy-start | bytes 4718596
  46.2 14.7 %copy-start.1 = (bf16[8,192,512]{2,1,0:T(8,128)(2,1)S(1)}, bf16[8,192,512]{2,1,0:T(8,128)(2,1)}, u32[]{:S(2)}) copy-start(bf16[8,192,512]{2,1,0:T(8,128)(2,1)} %backward_ref.1) | copy-start | bytes 4718596
  49.2 17.7 %collective-permute-start.12 = (bf16[8,64,128]{2,1,0:T(8,128)(2,1)S(1)}, bf16[8,64,128]{2,1,0:T(8,128)(2,1)S(1)}, u32[]{:S(2)}, u32[]{:S(2)}) collective-permute-start(bf16[8,64,128]{2,1,0:T(8,128)(2,1)S(1)} %get-tuple-element.29.refs_0_.own_ref), channel_id=1, source_target_pairs={{0,2},{4,6},{8,10},{12,14},{16,18},{20,22},{24,26},{28,30},{32,34}... | collective-permute-start | bytes 393224 | tf_op jit(solution)/shard_map/ppermute | solution.py:55
  49.3 17.6 %collective-permute-start.13 = (bf16[8,64,128]{2,1,0:T(8,128)(2,1)S(1)}, bf16[8,64,128]{2,1,0:T(8,128)(2,1)S(1)}, u32[]{:S(2)}, u32[]{:S(2)}) collective-permute-start(bf16[8,64,128]{2,1,0:T(8,128)(2,1)S(1)} %get-tuple-element.29.refs_0_.own_ref), channel_id=1, source_target_pairs={{2,4},{6,8},{10,12},{14,16},{18,20},{22,24},{26,28},{30,32},{34,36... | collective-permute-start | bytes 393224 | tf_op jit(solution)/shard_map/ppermute | solution.py:55
  57.6 12.4 %collective-permute-start.14 = (bf16[8,64,128]{2,1,0:T(8,128)(2,1)S(1)}, bf16[8,64,128]{2,1,0:T(8,128)(2,1)S(1)}, u32[]{:S(2)}, u32[]{:S(2)}) collective-permute-start(bf16[8,64,128]{2,1,0:T(8,128)(2,1)S(1)} %get-tuple-element.29.refs_0_.own_ref), channel_id=1, source_target_pairs={{4,8},{6,10},{12,16},{14,18},{20,24},{22,26},{28,32},{30,34},{36,4... | collective-permute-start | bytes 393224 | tf_op jit(solution)/shard_map/ppermute | solution.py:55
  60.7 9.6 %collective-permute-start.15 = (bf16[8,64,128]{2,1,0:T(8,128)(2,1)S(1)}, bf16[8,64,128]{2,1,0:T(8,128)(2,1)S(1)}, u32[]{:S(2)}, u32[]{:S(2)}) collective-permute-start(bf16[8,64,128]{2,1,0:T(8,128)(2,1)S(1)} %get-tuple-element.29.refs_0_.own_ref), channel_id=1, source_target_pairs={{0,4},{2,6},{8,12},{10,14},{16,20},{18,22},{24,28},{26,30},{32,36}... | collective-permute-start | bytes 393224 | tf_op jit(solution)/shard_map/ppermute | solution.py:55
